TPU v7x, 128 devices: a whole 4x4x4 slice. The times are simulated.
128 devices in a mesh: ctx: 32 (over z, y_lo, x), grp: 4 (over y_hi, core).
Axes of the slice: x: 4, y: 4 (y_hi: 2, y_lo: 2; y = y_hi * 2 + y_lo), z: 4, core: 2. Of those that a mesh axis runs over, the one named last changes fastest.
Arguments:
- query_input: bfloat16 [16384, 4096], P(('ctx', 'grp')), may hold values from -6 to 6
- key_input: bfloat16 [16384, 4096], P(('ctx', 'grp')), may hold values from -6 to 6
- value_input: bfloat16 [16384, 4096], P(('ctx', 'grp')), may hold values from -6 to 6
- out_grad: bfloat16 [16384, 4096], P(('ctx', 'grp')), may hold values from -6 to 6
- residues: float32 [8, 16], replicated, may hold values from -2 to 2
- decay_rates: float32 [8, 16], replicated, may hold values from 3.0517578e-06 to 0.15
Outputs:
- output: float32 [16384, 4096], P(('ctx', 'grp'))
- query_grad: float32 [16384, 4096], P(('ctx', 'grp'))
- key_grad: float32 [16384, 4096], P(('ctx', 'grp'))
- value_grad: float32 [16384, 4096], P(('ctx', 'grp'))
- residue_grad: float32 [8, 16], replicated
All inputs are finite; a program needn't handle non-finite values.
Results may differ from a plain program's by a relative error of at most 0.0055.
Values may be sent and summed in bfloat16 or wider, within the bound.
A program may use at most 192 MiB of HBM per device.

v0:
```python
import math

import jax
import jax.numpy as jnp
from jax import lax
from jax.sharding import PartitionSpec as P

GROUP = 512


HIGHEST = lax.Precision.HIGHEST


def entering(part, axis, combine, identity, reverse):
    count = lax.axis_size(axis)
    place = lax.axis_index(axis)
    ahead = count - 1 - place if reverse else place
    gathered = jax.tree.map(lambda a: lax.all_gather(a, axis), part)
    state = jax.tree.map(lambda a, e: jnp.zeros_like(a) + jnp.asarray(e, a.dtype), part, identity)

    def one(hop, state):
        source = count - 1 - hop if reverse else hop
        return combine(
            state, jax.tree.map(lambda a: lax.dynamic_index_in_dim(a, source, 0, False), gathered)
        )

    return lax.fori_loop(0, ahead, one, state)


def mode_tables(term_residues, decays, pairing, span):
    position = jnp.arange(span).astype(jnp.float32)
    distance = position[:, None] - position[None, :]
    causal_mask = distance >= 0.0
    lag_values = jnp.maximum(distance, 0.0)
    group_count = term_residues.shape[0]

    def one_mode(total, columns):
        res_column, decay_column = columns
        weight = jnp.where(
            causal_mask[None], jnp.exp(-decay_column[:, None, None] * lag_values[None]), 0.0
        )
        total = total + res_column[:, None, None] * weight
        return (total, jnp.sum(pairing * weight, axis=(1, 2)))

    start_total = jnp.zeros((group_count, span, span), jnp.float32)
    causal, inside = lax.scan(one_mode, start_total, (term_residues.T, decays.T))
    upper_part = causal.astype(jnp.bfloat16)
    lower_part = (causal - upper_part.astype(jnp.float32)).astype(jnp.bfloat16)
    return (upper_part, lower_part, inside.T)


def link_states(earlier, later):
    return (later[1][:, :, None] * earlier[0] + later[0], earlier[1] * later[1])


def convolve(product, inner_grad, term_residues, decays, carry_states):
    span, columns = product.shape
    group_count = columns // GROUP
    grouped = product.reshape(span, group_count, GROUP)
    grad_rows = inner_grad.reshape(span, group_count, GROUP)
    pairing = jnp.einsum("agc,bgc->gab", grad_rows, grouped, preferred_element_type=jnp.float32)
    upper_part, lower_part, inside = mode_tables(term_residues, decays, pairing, span)
    mixed_sum = jnp.einsum("gab,bgc->agc", upper_part, grouped, preferred_element_type=jnp.float32)
    mixed_sum = mixed_sum + jnp.einsum(
        "gab,bgc->agc", lower_part, grouped, preferred_element_type=jnp.float32
    )
    conv_sum = jnp.einsum("gab,agc->bgc", upper_part, grad_rows, preferred_element_type=jnp.float32)
    conv_sum = conv_sum + jnp.einsum(
        "gab,agc->bgc", lower_part, grad_rows, preferred_element_type=jnp.float32
    )
    position = jnp.arange(span).astype(jnp.float32)
    to_end = jnp.exp(-decays[:, :, None] * (span - 1.0 - position)[None, None, :])
    from_start = jnp.exp(-decays[:, :, None] * position[None, None, :])
    end_states = jnp.einsum("gmb,bgc->gmc", to_end, grouped.astype(jnp.float32), precision=HIGHEST)
    start_states = jnp.einsum(
        "gma,agc->gmc", from_start, grad_rows.astype(jnp.float32), precision=HIGHEST
    )
    factor = jnp.exp(-decays * float(span))
    carried_in, behind = carry_states(end_states, start_states, factor, span)
    rising = jnp.exp(-decays[:, :, None] * (position + 1.0)[None, None, :])
    falling = jnp.exp(-decays[:, :, None] * (span - position)[None, None, :])
    mixed_sum = mixed_sum + jnp.einsum(
        "gma,gmc->agc", term_residues[:, :, None] * rising, carried_in, precision=HIGHEST
    )
    conv_sum = conv_sum + jnp.einsum(
        "gmb,gmc->bgc", term_residues[:, :, None] * falling, behind, precision=HIGHEST
    )
    projected = jnp.einsum(
        "agc,gmc->gma", grad_rows.astype(jnp.float32), carried_in, precision=HIGHEST
    )
    residue_share = inside + jnp.sum(projected * rising, axis=2)
    return (mixed_sum.reshape(span, columns), conv_sum.reshape(span, columns), residue_share)


def finish(query_part, key_part, value_part, grad_part, mixed_out, conv_grad):
    output = query_part.astype(jnp.float32) * mixed_out
    query_grad = grad_part.astype(jnp.float32) * mixed_out
    key_grad = conv_grad * value_part.astype(jnp.float32)
    value_grad = conv_grad * key_part.astype(jnp.float32)
    return (output, query_grad, key_grad, value_grad)


def gated_inputs(query_input, key_input, value_input, out_grad):
    product = (key_input.astype(jnp.float32) * value_input.astype(jnp.float32)).astype(jnp.bfloat16)
    inner_grad = (out_grad.astype(jnp.float32) * query_input.astype(jnp.float32)).astype(
        jnp.bfloat16
    )
    return (product, inner_grad)


def channel_layout(query_input, key_input, value_input, out_grad, residues, decay_rates):
    product, inner_grad = gated_inputs(query_input, key_input, value_input, out_grad)
    prod_cols, grad_cols = (
        lax.all_to_all(product, "grp", split_axis=1, concat_axis=0, tiled=True),
        lax.all_to_all(inner_grad, "grp", split_axis=1, concat_axis=0, tiled=True),
    )
    row_count, columns = prod_cols.shape
    group_count = columns // GROUP
    first_group = lax.axis_index("grp") * group_count
    local_res = lax.dynamic_slice_in_dim(residues, first_group, group_count, 0)
    local_decay = lax.dynamic_slice_in_dim(decay_rates, first_group, group_count, 0)

    def carry_states(end_states, start_states, factor, span):
        neutral = (jnp.zeros_like(end_states), jnp.ones_like(factor))
        carried_in, spent_ahead = entering((end_states, factor), "ctx", link_states, neutral, False)
        behind, spent_behind = entering((start_states, factor), "ctx", link_states, neutral, True)
        return (carried_in, behind)

    mixed_cols, conv_cols, residue_share = convolve(
        prod_cols, grad_cols, local_res, local_decay, carry_states
    )
    mixed_rows, conv_rows = (
        lax.all_to_all(mixed_cols, "grp", split_axis=0, concat_axis=1, tiled=True),
        lax.all_to_all(conv_cols, "grp", split_axis=0, concat_axis=1, tiled=True),
    )
    results = finish(query_input, key_input, value_input, out_grad, mixed_rows, conv_rows)
    placed = lax.dynamic_update_slice_in_dim(
        jnp.zeros(residues.shape, jnp.float32), residue_share, first_group, 0
    )
    return (results, placed, row_count * lax.axis_size("ctx"))


def on_device(query_input, key_input, value_input, out_grad, residues, decay_rates):
    results, placed, length = channel_layout(
        query_input, key_input, value_input, out_grad, residues, decay_rates
    )
    summed = lax.psum(placed, ("ctx", "grp"))
    residue_grad = summed / (length * math.sqrt(GROUP))
    return (results[0], results[1], results[2], results[3], residue_grad)


def solution(mesh):
    in_specs = (
        P(("ctx", "grp"), None),
        P(("ctx", "grp"), None),
        P(("ctx", "grp"), None),
        P(("ctx", "grp"), None),
        P(),
        P(),
    )
    out_specs = (
        P(("ctx", "grp"), None),
        P(("ctx", "grp"), None),
        P(("ctx", "grp"), None),
        P(("ctx", "grp"), None),
        P(),
    )
    return jax.shard_map(
        on_device, mesh=mesh, in_specs=in_specs, out_specs=out_specs, check_vma=False
    )
```

profile of v0, /device:TPU:1, one launch (start us, length us, event | category | flops | bytes accessed | tf_op | source)
XLA Modules:
  0.0 491.0 jit_solution(2044057091201564266)
XLA Ops:
  7.2 1.8 fusion.5
  9.0 1.1 copy.101
  10.0 6.0 %all-to-all-start.1 = ((bf16[128,4,1024]{2,0,1:T(8,128)(2,1)}), bf16[128,4,1024]{2,0,1:T(8,128)(2,1)S(1)}, u32[]{:S(2)}, u32[]{:S(2)}) async-start(bf16[128,4,1024]{2,0,1:T(8,128)(2,1)} %bitcast.53), calls=%async_computation.1 | async-start | bytes 2097152 | tf_op jit(solution)/shard_map/all_to_all | solution.py:115
  16.9 14.2 %all-to-all-done.1 = bf16[128,4,1024]{2,0,1:T(8,128)(2,1)S(1)} async-done(((bf16[128,4,1024]{2,0,1:T(8,128)(2,1)}), bf16[128,4,1024]{2,0,1:T(8,128)(2,1)S(1)}, u32[]{:S(2)}, u32[]{:S(2)}) %all-to-all-start.1) | async-done | bytes 1048608 | tf_op jit(solution)/shard_map/all_to_all | solution.py:115
  32.1 1.8 reshape.76
  33.9 1.2 fusion.12
  36.5 5.1 %all-to-all-start = ((bf16[128,4,1024]{2,0,1:T(8,128)(2,1)}), bf16[128,4,1024]{2,0,1:T(8,128)(2,1)}, u32[]{:S(2)}, u32[]{:S(2)}) async-start(bf16[128,4,1024]{2,0,1:T(8,128)(2,1)} %bitcast.54), calls=%async_computation | async-start | bytes 2097152 | tf_op jit(solution)/shard_map/all_to_all | solution.py:114
  41.7 68.3 %all-gather.3 = f32[32,2,16]{2,1,0:T(2,128)S(1)} all-gather(f32[1,2,16]{2,1,0:T(2,128)S(1)} %get-tuple-element.293), channel_id=2, replica_groups=mesh['ctx'=32,'grp'=4] {'ctx'}, dimensions={0}, use_global_device_ids=true | all-gather | bytes 4224 | tf_op jit(solution)/shard_map/all_gather | solution.py:18
  110.1 2.6 reshape.75
  112.7 2.4 fusion.7
  115.1 3.3 fusion.9
  118.4 54.7 %while.43 = (s32[]{:T(128)}, f32[2,512,512]{2,1,0:T(8,128)S(1)}, f32[16,2]{1,0:T(8,128)S(1)}, f32[16,2]{1,0:T(8,128)S(1)}, f32[16,2]{1,0:T(8,128)S(1)}, /*index=...) while((s32[]{:T(128)}, f32[2,512,512]{2,1,0:T(8,128)S(1)}, ...), condition=%wide.region_2.3_spmd.clone.clone.clone, body=%wide.region_0.2_spmd.clone.clone.clone.sunk | while | flops 4718595 | bytes 8917183 | solution.py:46
  118.9 3.0 multiply_reduce_fusion.2
  122.3 3.0 multiply_reduce_fusion.2
  125.7 3.0 multiply_reduce_fusion.2
  129.1 3.0 multiply_reduce_fusion.2
  132.5 3.0 multiply_reduce_fusion.2
  135.9 3.0 multiply_reduce_fusion.2
  139.4 3.0 multiply_reduce_fusion.2
  142.8 3.0 multiply_reduce_fusion.2
  146.2 3.0 multiply_reduce_fusion.2
  149.6 3.0 multiply_reduce_fusion.2
  153.0 3.0 multiply_reduce_fusion.2
  156.4 3.0 multiply_reduce_fusion.2
  159.9 3.0 multiply_reduce_fusion.2
  163.3 3.0 multiply_reduce_fusion.2
  166.7 3.0 multiply_reduce_fusion.2
  170.1 3.0 multiply_reduce_fusion.2
  173.1 2.5 copy.78
  175.6 3.7 copy.71
  179.2 3.4 fusion.39
  182.6 2.0 fusion.43
  184.7 2.1 fusion.41
  186.7 2.1 fusion.44
  188.8 28.8 %while.42 = (s32[]{:T(128)}, f32[2,16,512]{2,1,0:T(8,128)S(1)}, s32[]{:T(128)}, f32[32,2,16]{2,1,0:T(2,128)S(1)}, f32[32,2,16,512]{3,2,1,0:T(8,128)}, /*index=5*/s32[]{:T(128)}, s32[]{:T(128)}, s32[]{:T(128)}, s32[]{:T(128)}) while((s32[]{:T(128)}, f32[2,16,512]{2,1,0:T(8,128)S(1)}, s32[]{:T(128)}, f32[32,2,16]{2,1,0:T(2,128)S(1)}, ...), condition=%wide.region_6.7_spmd, body=%wide.region_5.6_spmd.sunk | while | flops 32774 | bytes 197147 | solution.py:27
  217.6 5.5 %add_bitcast_fusion = f32[512,2,512]{0,2,1:T(8,128)} fusion(f32[2,512,512]{2,1,0:T(8,128)} %fusion.39, f32[2,512,512]{2,1,0:T(8,128)} %fusion.43, f32[2,16,512]{2,1,0:T(8,128)S(1)} %get-tuple-element.178, f32[512]{0:T(512)S(1)} %fusion.35, f32[2,16]{1,0:T(2,128)S(1)} %constant_dynamic-slice_fusion.1, f32[2,16]{1,0:T(2,128)S(1)} %get-tuple-element.294), kind=kOutput, calls=%fused_computation.21 | convolution fusion | flops 101744640 | bytes 6359296 | tf_op jit(solution)/shard_map/gmb,gmc->bgc/dot_general | solution.py:85
  223.1 1.9 all_to_all.62
  225.0 1.5 copy.81
  226.5 18.8 %all-to-all-start.3 = ((f32[4,128,1024]{1,2,0:T(8,128)}), f32[4,128,1024]{1,2,0:T(8,128)S(1)}, u32[]{:S(2)}, u32[]{:S(2)}) async-start(f32[4,128,1024]{1,2,0:T(8,128)} %copy.81), calls=%async_computation.3 | async-start | bytes 4194304 | tf_op jit(solution)/shard_map/all_to_all | solution.py:134
  245.3 77.5 %all-gather.7.cloned.1.call-done = f32[64,16,512]{2,1,0:T(8,128)} async-done(((f32[2,16,512]{2,1,0:T(8,128)}), f32[64,16,512]{2,1,0:T(8,128)}) %all-gather.7.cloned.1.call-update) | async-done | bytes 2097168 | tf_op jit(solution)/shard_map/all_gather | solution.py:18
  322.9 5.5 %add_bitcast_fusion.1 = f32[512,2,512]{0,2,1:T(8,128)} fusion(f32[2,512,512]{2,1,0:T(8,128)} %fusion.41, f32[2,512,512]{2,1,0:T(8,128)} %fusion.44, f32[2,16,512]{2,1,0:T(8,128)S(1)} %get-tuple-element.177, f32[512]{0:T(512)S(1)} %fusion.33, f32[2,16]{1,0:T(2,128)S(1)} %constant_dynamic-slice_fusion.1, f32[2,16]{1,0:T(2,128)S(1)} %get-tuple-element.294), kind=kOutput, calls=%fused_computation.22 | convolution fusion | flops 101744640 | bytes 6359296 | tf_op jit(solution)/shard_map/gma,gmc->agc/dot_general | solution.py:82
  328.4 2.9 all_to_all.58
  331.2 3.0 copy.75
  334.3 26.2 %all-to-all-start.2 = ((f32[4,128,1024]{1,2,0:T(8,128)}), f32[4,128,1024]{1,2,0:T(8,128)}, u32[]{:S(2)}, u32[]{:S(2)}) async-start(f32[4,128,1024]{1,2,0:T(8,128)} %copy.75), calls=%async_computation.2 | async-start | bytes 4194304 | tf_op jit(solution)/shard_map/all_to_all | solution.py:133
  361.6 110.7 %psum.7 = f32[8,16]{1,0:T(8,128)S(1)} all-reduce(f32[8,16]{1,0:T(8,128)S(1)} %fusion.36), channel_id=1, replica_groups=mesh['ctx'=32,'grp'=4] {'ctx','grp'}, use_global_device_ids=true, to_apply=%region_8.9 | all-reduce | flops 128 | bytes 1024 | tf_op jit(solution)/shard_map/psum | solution.py:147
  472.9 1.8 copy.82
  474.8 3.0 copy.76
  477.8 6.3 %convert_multiply_fusion = (f32[128,4096]{1,0:T(8,128)}, f32[128,4096]{1,0:T(8,128)}, f32[128,4096]{1,0:T(8,128)}, f32[128,4096]{1,0:T(8,128)}) fusion(f32[128,4096]{1,0:T(8,128)} %copy.76, bf16[128,4096]{1,0:T(8,128)(2,1)} %param.15, bf16[128,4096]{1,0:T(8,128)(2,1)} %param.12, f32[128,4096]{1,0:T(8,128)S(1)} %copy-done.3, ...), kind=kLoop, calls=%fused_computation.13 | loop fusion | flops 4194304 | bytes 16777216 | tf_op jit(solution)/shard_map/mul | solution.py:97
  (170 shorter events, 40.5 us)
Async XLA Ops:
  7.2 34.5 %copy-start = (f32[8,16]{1,0:T(8,128)S(1)}, f32[8,16]{1,0:T(8,128)}, u32[]{:S(2)}) copy-start(f32[8,16]{1,0:T(8,128)} %param.16) | copy-start | bytes 1540
  10.0 21.1 %all-to-all-start.1 = ((bf16[128,4,1024]{2,0,1:T(8,128)(2,1)}), bf16[128,4,1024]{2,0,1:T(8,128)(2,1)S(1)}, u32[]{:S(2)}, u32[]{:S(2)}) async-start(bf16[128,4,1024]{2,0,1:T(8,128)(2,1)} %bitcast.53), calls=%async_computation.1 | async-start | bytes 2097152 | tf_op jit(solution)/shard_map/all_to_all | solution.py:115
  16.0 19.1 %copy-start.4 = (bf16[128,4096]{1,0:T(8,128)(2,1)S(1)}, bf16[128,4096]{1,0:T(8,128)(2,1)}, u32[]{:S(2)}) copy-start(bf16[128,4096]{1,0:T(8,128)(2,1)} %param.14) | copy-start | bytes 3145732
  16.0 19.2 %copy-start.6 = (bf16[128,4096]{1,0:T(8,128)(2,1)S(1)}, bf16[128,4096]{1,0:T(8,128)(2,1)}, u32[]{:S(2)}) copy-start(bf16[128,4096]{1,0:T(8,128)(2,1)} %param.13) | copy-start | bytes 3145732
  16.0 172.8 %all-gather.9.cloned.1.call-start = ((), (), s32[]{:S(2)}) async-start(), calls=%async_computation.5 | async-start | bytes 2162688 | tf_op jit(solution)/shard_map/all_gather | solution.py:18
  31.1 1.0 copy-start.7
  36.5 73.6 %all-to-all-start = ((bf16[128,4,1024]{2,0,1:T(8,128)(2,1)}), bf16[128,4,1024]{2,0,1:T(8,128)(2,1)}, u32[]{:S(2)}, u32[]{:S(2)}) async-start(bf16[128,4,1024]{2,0,1:T(8,128)(2,1)} %bitcast.54), calls=%async_computation | async-start | bytes 2097152 | tf_op jit(solution)/shard_map/all_to_all | solution.py:114
  41.6 281.3 %all-gather.7.cloned.1.call-start = ((), (), s32[]{:S(2)}) async-start(), calls=%async_computation.4 | async-start | bytes 2162688 | tf_op jit(solution)/shard_map/all_gather | solution.py:18
  179.2 3.4 copy-start.2
  182.6 2.1 copy-start.1
  226.5 107.8 %all-to-all-start.3 = ((f32[4,128,1024]{1,2,0:T(8,128)}), f32[4,128,1024]{1,2,0:T(8,128)S(1)}, u32[]{:S(2)}, u32[]{:S(2)}) async-start(f32[4,128,1024]{1,2,0:T(8,128)} %copy.81), calls=%async_computation.3 | async-start | bytes 4194304 | tf_op jit(solution)/shard_map/all_to_all | solution.py:134
  334.3 140.5 %all-to-all-start.2 = ((f32[4,128,1024]{1,2,0:T(8,128)}), f32[4,128,1024]{1,2,0:T(8,128)}, u32[]{:S(2)}, u32[]{:S(2)}) async-start(f32[4,128,1024]{1,2,0:T(8,128)} %copy.75), calls=%async_computation.2 | async-start | bytes 4194304 | tf_op jit(solution)/shard_map/all_to_all | solution.py:133
  474.8 3.0 copy-start.3
  474.8 3.0 copy-start.5
Sparse Core Ops, SparseCore 0:
  35.3 132.3 all-gather.8
  169.3 153.5 all-gather.6
where the time goes:
time: 494 us; the launch traced here: 491 us
  blocking collectives  179 us (36%)
  other arithmetic  91.8 us (19%)
  waiting for transfers between devices  91.8 us (19%)
  starting transfers between devices  56.1 us (11%)
  local copies, waits for them, and re-layouts  28.8 us (6%)
  matrix products  28.5 us (6%)
  between operations  14.1 us (3%)
    psum x1, blocking collectives, on_device(): summed = lax.psum(placed, ('ctx', 'grp'))  111 us
    all_gather x2, waiting for transfers between devices, entering(): gathered = jax.tree.map(lambda a: lax.all_gather(a, axis), part)  77.6 us
    all_gather x1, blocking collectives, entering(): gathered = jax.tree.map(lambda a: lax.all_gather(a, axis), part)  68.3 us
    reduce_sum x16, other arithmetic, one_mode(): return (total, jnp.sum(pairing * weight, axis=(1, 2)))  47.3 us
    add x31, other arithmetic, link_states(): return (later[1][:, :, None] * earlier[0] + later[0], earlier[1] * later[1])  28.6 us
    all_to_all x1, starting transfers between devices, channel_layout(): lax.all_to_all(mixed_cols, 'grp', split_axis=0, concat_axis=1, tiled=True)  26.2 us
    all_to_all x1, starting transfers between devices, channel_layout(): lax.all_to_all(conv_cols, 'grp', split_axis=0, concat_axis=1, tiled=True)  18.8 us
    all_to_all x1, waiting for transfers between devices, channel_layout(): lax.all_to_all(inner_grad, 'grp', split_axis=1, concat_axis=0, tiled=True)  14.2 us
  transfers between devices with their start and end apart: 6, of which 2 were waited for; matrix products, arithmetic and copies ran while one was open for 26% of the time, Pallas kernels for 0%

commit v1 on v0

v1 whole, which is shorter than its diff:
```python
import math

import jax
import jax.numpy as jnp
from jax import lax
from jax.experimental import pallas as pl
from jax.experimental.pallas import tpu as pltpu
from jax.sharding import PartitionSpec as P

GROUP = 512
MODES = 16
LANES = 128
MESH = pl.DeviceIdType.MESH


def iota(shape, axis):
    return lax.broadcasted_iota(jnp.int32, shape, axis)


def split(x):
    hi = x.astype(jnp.bfloat16)
    lo = (x - hi.astype(jnp.float32)).astype(jnp.bfloat16)
    return hi, lo


def column(row):
    eye = iota((MODES, MODES), 0) == iota((MODES, MODES), 1)
    return jnp.sum(jnp.where(eye, jnp.broadcast_to(row, (MODES, MODES)), 0.0), axis=1, keepdims=True)


def gated(a, b):
    return (a.astype(jnp.float32) * b.astype(jnp.float32)).astype(jnp.bfloat16)


def exchange_kernel(
    count, groups, span, inner,
    q_hbm, k_hbm, v_hbm, o_hbm, decay_ref,
    state_ref, total_ref,
    ins, prod, grad, send, recv, back, acol, vbuf, v_one, v_two, v_three,
    load_sem, sems,
):
    me = lax.axis_index("ctx") * inner + lax.axis_index("grp")

    def place(j):
        return (lax.div(j, inner), lax.rem(j, inner))

    sources = (q_hbm, k_hbm, v_hbm, o_hbm)

    def load(g, n):
        return pltpu.make_async_copy(
            sources[n].at[:, pl.ds(pl.multiple_of(g * GROUP, GROUP), GROUP)],
            ins.at[n, g],
            load_sem.at[g, n],
        )

    for g in range(groups):
        for n in range(4):
            load(g, n).start()

    barrier = pltpu.get_barrier_semaphore()

    def greet(d, c):
        pl.semaphore_signal(
            barrier, inc=1, device_id=place(lax.rem(me + d, count)), device_id_type=MESH
        )
        return c

    lax.fori_loop(1, count, greet, 0)

    lane = iota((MODES, LANES), 1).astype(jnp.float32)

    for g in range(groups):
        rates = jnp.broadcast_to(column(decay_ref[g : g + 1, :]), (MODES, LANES))
        acol[g * MODES : (g + 1) * MODES, :] = rates

    def states(g, c):
        for n in range(4):
            load(g, n).wait()
        p = gated(ins[1, g], ins[2, g])
        r = gated(ins[3, g], ins[0, g])
        prod[g] = p
        grad[g] = r
        rates = acol[pl.ds(pl.multiple_of(g * MODES, MODES), MODES), :]
        to_end = jnp.concatenate(split(jnp.exp(-rates * (span - 1.0 - lane))), axis=0)
        from_start = jnp.concatenate(split(jnp.exp(-rates * lane)), axis=0)
        ends = jnp.dot(to_end, p, preferred_element_type=jnp.float32)
        starts = jnp.dot(from_start, r, preferred_element_type=jnp.float32)
        ends = ends[:MODES] + ends[MODES:]
        starts = starts[:MODES] + starts[MODES:]
        for k in range(4):
            send[pl.ds(g * 128 + k, MODES, stride=8), :] = ends[:, k * LANES : (k + 1) * LANES]
            send[pl.ds(g * 128 + 4 + k, MODES, stride=8), :] = starts[:, k * LANES : (k + 1) * LANES]
        return c

    lax.fori_loop(0, groups, states, 0)

    def tile(ref, j):
        return ref.at[pl.ds(pl.multiple_of(j * 8, 8), 8), :]

    def scatter(source, target, send_sem, recv_sem):
        def one(d, c):
            j = lax.rem(me + d, count)
            pltpu.make_async_remote_copy(
                src_ref=tile(source, j),
                dst_ref=tile(target, me),
                send_sem=send_sem,
                recv_sem=recv_sem,
                device_id=place(j),
                device_id_type=MESH,
            ).start()
            return c

        lax.fori_loop(1, count, one, 0)

    def await_all(ref, sem):
        part = ref.at[pl.ds(0, (count - 1) * 8), :]
        pltpu.make_async_copy(part, part, sem).wait()

    pl.semaphore_wait(barrier, count - 1)
    scatter(send, recv, sems.at[0], sems.at[1])

    row = iota((span, LANES), 0)
    col = iota((span, LANES), 1)
    flip = (row + col == span - 1).astype(jnp.bfloat16)
    here = iota((MODES, LANES), 1) - iota((MODES, LANES), 0)

    def pairs(g, total):
        pair = lax.dot_general(
            prod[g], grad[g], (((1,), (1,)), ((), ())), preferred_element_type=jnp.float32
        )
        hi, lo = split(pair)
        turned = jnp.dot(hi, flip, preferred_element_type=jnp.float32) + jnp.dot(
            lo, flip, preferred_element_type=jnp.float32
        )
        lagged = pltpu.roll(turned, 0, 1, stride=1, stride_axis=0)
        cross = jnp.sum(jnp.where(col >= row, lagged, 0.0), axis=0, keepdims=True)
        rates = acol[pl.ds(pl.multiple_of(g * MODES, MODES), MODES), :]
        inside = jnp.sum(jnp.exp(-rates * (span - 1.0 - lane)) * cross, axis=1, keepdims=True)
        return total + jnp.sum(jnp.where(here == g * MODES, inside, 0.0), axis=0, keepdims=True)

    share = lax.fori_loop(0, groups, pairs, jnp.zeros((1, LANES), jnp.float32))

    mine = pl.ds(pl.multiple_of(me * 8, 8), 8)
    await_all(recv, sems.at[1])
    recv[mine, :] = send[mine, :]

    rate = jnp.broadcast_to(acol[pl.ds(me, 1), :], (4, LANES))
    factor = jnp.exp(-rate * float(span))
    zero = jnp.zeros((4, LANES), jnp.float32)

    def step(i, carry):
        rising, falling, acc = carry
        up = pl.multiple_of(i * 8, 8)
        down = pl.multiple_of((count - 1 - i) * 8, 8)
        back[pl.ds(up, 4), :] = rising
        back[pl.ds(down + 4, 4), :] = falling
        acc = acc + rising * recv[pl.ds(up + 4, 4), :]
        rising = factor * rising + recv[pl.ds(up, 4), :]
        falling = factor * falling + recv[pl.ds(down + 4, 4), :]
        return rising, falling, acc

    rising, falling, acc = lax.fori_loop(0, count, step, (zero, zero, zero), unroll=8)
    total = jnp.sum(jnp.sum(jnp.exp(-rate) * acc, axis=0, keepdims=True), axis=1, keepdims=True)
    mode = iota((1, LANES), 1) == me
    share = share + jnp.where(mode, jnp.broadcast_to(total, (1, LANES)), 0.0)

    def reduce(buf, radix, stride, value, sem, out_sem, work=None):
        digit = lax.rem(lax.div(me, stride), radix)
        base = me - digit * stride
        vbuf[sem // 2] = value
        copies = []
        for d in range(1, radix):
            other = lax.rem(digit + d, radix)
            copy = pltpu.make_async_remote_copy(
                src_ref=vbuf.at[sem // 2],
                dst_ref=buf.at[digit],
                send_sem=sems.at[sem],
                recv_sem=sems.at[out_sem],
                device_id=place(base + other * stride),
                device_id_type=MESH,
            )
            copy.start()
        if work is not None:
            work()
        part = buf.at[pl.ds(0, radix - 1)]
        pltpu.make_async_copy(part, part, sems.at[out_sem]).wait()
        buf[digit] = value
        summed = jnp.sum(buf[...], axis=0)
        pltpu.make_async_copy(part, part, sems.at[sem]).wait()
        return summed

    def phase_two():
        scatter(back, state_ref, sems.at[2], sems.at[3])
        state_ref[mine, :] = back[mine, :]

    share = reduce(v_one, 4, 1, share, 4, 5, phase_two)
    share = reduce(v_two, 8, 4, share, 6, 7)
    share = reduce(v_three, 4, 32, share, 8, 9)
    total_ref[...] = share
    await_all(send, sems.at[0])
    await_all(back, sems.at[2])
    await_all(state_ref, sems.at[3])


def exchange(query_input, key_input, value_input, out_grad, decays):
    inner = lax.axis_size("grp")
    count = lax.axis_size("ctx") * inner
    span, width = query_input.shape
    groups = width // GROUP
    rows = count * 8
    f32 = jnp.float32
    bf16 = jnp.bfloat16

    def body(*refs):
        exchange_kernel(count, groups, span, inner, *refs)

    hbm = pl.BlockSpec(memory_space=pl.ANY)
    vmem = pl.BlockSpec(memory_space=pltpu.VMEM)
    return pl.pallas_call(
        body,
        out_shape=(
            jax.ShapeDtypeStruct((rows, LANES), f32),
            jax.ShapeDtypeStruct((1, LANES), f32),
        ),
        in_specs=[hbm] * 4 + [vmem],
        out_specs=(vmem, vmem),
        scratch_shapes=[
            pltpu.VMEM((4, groups, span, GROUP), bf16),
            pltpu.VMEM((groups, span, GROUP), bf16),
            pltpu.VMEM((groups, span, GROUP), bf16),
            pltpu.VMEM((rows, LANES), f32),
            pltpu.VMEM((rows, LANES), f32),
            pltpu.VMEM((rows, LANES), f32),
            pltpu.VMEM((groups * MODES, LANES), f32),
            pltpu.VMEM((5, 1, LANES), f32),
            pltpu.VMEM((4, 1, LANES), f32),
            pltpu.VMEM((8, 1, LANES), f32),
            pltpu.VMEM((4, 1, LANES), f32),
            pltpu.SemaphoreType.DMA((groups, 4)),
            pltpu.SemaphoreType.DMA((10,)),
        ],
        compiler_params=pltpu.CompilerParams(
            collective_id=0, has_side_effects=True, vmem_limit_bytes=40 * 1024 * 1024
        ),
    )(query_input, key_input, value_input, out_grad, decays)


def finish_kernel(
    span, scale,
    q_ref, k_ref, v_ref, o_ref, state_ref, total_ref, res_ref, decay_ref,
    out_ref, qg_ref, kg_ref, vg_ref, rg_ref,
):
    g = pl.program_id(0)
    q, k, v, o = (ref[...].astype(jnp.float32) for ref in (q_ref, k_ref, v_ref, o_ref))
    p = (k * v).astype(jnp.bfloat16)
    r = (o * q).astype(jnp.bfloat16)
    decay_row = decay_ref[pl.ds(g, 1), :]
    res_row = res_ref[pl.ds(g, 1), :]
    rates = column(decay_row)
    weights = column(res_row)
    lane_i = iota((MODES, LANES), 1)
    lane = lane_i.astype(jnp.float32)
    turned = jnp.where(lane_i == 0, 0, LANES - lane_i).astype(jnp.float32)
    row = iota((span, LANES), 0)
    col = iota((span, LANES), 1)

    def toeplitz(lags, keep):
        line = jnp.sum(weights * jnp.exp(-rates * lags), axis=0, keepdims=True)
        full = pltpu.roll(jnp.broadcast_to(line, (span, LANES)), 0, 1, stride=1, stride_axis=0)
        return split(jnp.where(keep, full, 0.0))

    down_hi, down_lo = toeplitz(turned, row >= col)
    up_hi, up_lo = toeplitz(lane, row <= col)

    def dot(a, b):
        return jnp.dot(a, b, preferred_element_type=jnp.float32)

    token = iota((span, MODES), 0).astype(jnp.float32)
    rise = split(res_row * jnp.exp(-decay_row * (token + 1.0)))
    fall = split(res_row * jnp.exp(-decay_row * (span - token)))

    def carried(table, first):
        state = jnp.concatenate(
            [state_ref[pl.ds(first + n, MODES, stride=8), :] for n in range(4)], axis=1
        )
        hi, lo = split(state)
        return dot(table[0], hi) + dot(table[0], lo) + dot(table[1], hi)

    mixed = dot(down_hi, p) + dot(down_lo, p) + carried(rise, 0)
    out_ref[...] = q * mixed
    qg_ref[...] = o * mixed
    conv = dot(up_hi, r) + dot(up_lo, r) + carried(fall, 4)
    kg_ref[...] = conv * v
    vg_ref[...] = conv * k

    @pl.when(g == 0)
    def _():
        groups = rg_ref.shape[0]
        spread = jnp.broadcast_to(total_ref[...], (groups, LANES))
        own = lax.div(iota((groups, LANES), 1), MODES) == iota((groups, LANES), 0)
        spread = jnp.where(own, spread, 0.0)
        out = spread
        for n in range(1, groups):
            out = out + pltpu.roll(spread, LANES - n * MODES, 1)
        rg_ref[...] = out[:, :MODES] * scale


def finish(query_input, key_input, value_input, out_grad, state, total, residues, decays, length):
    span, width = query_input.shape
    groups = width // GROUP
    scale = 1.0 / (length * math.sqrt(GROUP))

    def body(*refs):
        finish_kernel(span, scale, *refs)

    block = pl.BlockSpec((span, GROUP), lambda g: (0, g))
    small = pl.BlockSpec(residues.shape, lambda g: (0, 0))
    big = jax.ShapeDtypeStruct((span, width), jnp.float32)
    return pl.pallas_call(
        body,
        grid=(groups,),
        out_shape=(big, big, big, big, jax.ShapeDtypeStruct(residues.shape, jnp.float32)),
        in_specs=[block] * 4
        + [
            pl.BlockSpec((MODES * 8, LANES), lambda g: (g, 0)),
            pl.BlockSpec((1, LANES), lambda g: (0, 0)),
            small,
            small,
        ],
        out_specs=(block, block, block, block, small),
        compiler_params=pltpu.CompilerParams(
            dimension_semantics=("arbitrary",), vmem_limit_bytes=40 * 1024 * 1024
        ),
    )(query_input, key_input, value_input, out_grad, state, total, residues, decays)


def on_device(query_input, key_input, value_input, out_grad, residues, decay_rates):
    length = query_input.shape[0] * lax.axis_size("ctx") * lax.axis_size("grp")
    state, total = exchange(query_input, key_input, value_input, out_grad, decay_rates)
    return finish(
        query_input, key_input, value_input, out_grad, state, total, residues, decay_rates, length
    )


def solution(mesh):
    rows = P(("ctx", "grp"), None)
    return jax.shard_map(
        on_device,
        mesh=mesh,
        in_specs=(rows, rows, rows, rows, P(), P()),
        out_specs=(rows, rows, rows, rows, P()),
        check_vma=False,
    )
```

time: 494 us -> 46.9 us (0.09)
  blocking collectives: 179 us -> 0 us
  other arithmetic: 91.8 us -> 0 us
  waiting for transfers between devices: 91.8 us -> 0 us
  starting transfers between devices: 56.1 us -> 0 us
  Pallas kernels: 0 us -> 40 us
  matrix products: 28.5 us -> 0 us
  local copies, waits for them, and re-layouts: 28.8 us -> 5.58 us
  between operations: 14.1 us -> 0.66 us
    psum x1 -> x0, blocking collectives: 111 us -> none  [on_device(): summed = lax.psum(placed, ('ctx', 'grp'))]
    all_gather x2 -> x0, waiting for transfers between devices: 77.6 us -> none  [entering(): gathered = jax.tree.map(lambda a: lax.all_gather(a, axis), part)]
    all_gather x1 -> x0, blocking collectives: 68.3 us -> none  [entering(): gathered = jax.tree.map(lambda a: lax.all_gather(a, axis), part)]
    all_to_all x4 -> x0, starting transfers between devices: 56.1 us -> none  [the longest x1 26.2 us: channel_layout(): lax.all_to_all(mixed_cols, 'grp', split_axis=0, concat_axis=1, tiled=True)]
    reduce_sum x16 -> x0, other arithmetic: 47.3 us -> none  [one_mode(): return (total, jnp.sum(pairing * weight, axis=(1, 2)))]
    pallas_call x0 -> x2, Pallas kernels: none -> 40 us  [the longest x1 32.6 us: exchange(): pl.pallas_call(body, out_shape=(jax.ShapeDtypeStruct((rows, LANES), f32),...]
    add x32 -> x0, other arithmetic: 28.6 us -> none  [the longest x31 28.6 us: link_states(): return (later[1][:, :, None] * earlier[0] + later[0], earlier[1] * later[1])]
    dot_general x10 -> x0, matrix products: 28.5 us -> none  [the longest x1 5.47 us: convolve(): jnp.einsum('gma,gmc->agc', term_residues[:, :, None] * rising, carried_in...]
  transfers between devices with their start and end apart: 6 -> 0, of which waited for: 2 -> 0; matrix products, arithmetic and copies ran while one was open for 26% -> 0% of each run, Pallas kernels for 0% -> 0%
where the time goes in v1:
time: 46.9 us; the launch traced here: 46.3 us
  Pallas kernels  40 us (85%)
  local copies, waits for them, and re-layouts  5.58 us (12%)
  between operations  0.66 us (1%)
    pallas_call x1, Pallas kernels, exchange(): pl.pallas_call(body, out_shape=(jax.ShapeDtypeStruct((rows, LANES), f32),...  32.6 us
    pallas_call x1, Pallas kernels, finish(): pl.pallas_call(body, grid=(groups,), out_shape=(big, big, big, big, jax.S...  7.45 us
    unnamed x12, local copies, waits for them, and re-layouts  5.58 us

profile of v1, /device:TPU:1, one launch (start us, length us, event | category | flops | bytes accessed | tf_op | source)
XLA Modules:
  0.0 46.3 jit_solution(9573090715046875253)
XLA Ops:
  0.6 0.0 copy-start
  0.6 1.2 %copy-done = bf16[128,4096]{1,0:T(8,128)(2,1)S(1)} copy-done((bf16[128,4096]{1,0:T(8,128)(2,1)S(1)}, bf16[128,4096]{1,0:T(8,128)(2,1)}, u32[]{:S(2)}) %copy-start) | copy-done | bytes 1048600
  1.9 0.0 copy-start.1
  1.9 1.2 %copy-done.1 = bf16[128,4096]{1,0:T(8,128)(2,1)S(1)} copy-done((bf16[128,4096]{1,0:T(8,128)(2,1)S(1)}, bf16[128,4096]{1,0:T(8,128)(2,1)}, u32[]{:S(2)}) %copy-start.1) | copy-done | bytes 1048600
  3.1 0.0 copy-start.2
  3.1 1.2 %copy-done.2 = bf16[128,4096]{1,0:T(8,128)(2,1)S(1)} copy-done((bf16[128,4096]{1,0:T(8,128)(2,1)S(1)}, bf16[128,4096]{1,0:T(8,128)(2,1)}, u32[]{:S(2)}) %copy-start.2) | copy-done | bytes 1048600
  4.3 0.0 copy-start.3
  4.3 1.2 %copy-done.3 = bf16[128,4096]{1,0:T(8,128)(2,1)S(1)} copy-done((bf16[128,4096]{1,0:T(8,128)(2,1)S(1)}, bf16[128,4096]{1,0:T(8,128)(2,1)}, u32[]{:S(2)}) %copy-start.3) | copy-done | bytes 1048600
  5.5 0.0 copy-start.4
  5.5 0.7 %copy-done.4 = f32[8,16]{1,0:T(8,128)S(1)} copy-done((f32[8,16]{1,0:T(8,128)S(1)}, f32[8,16]{1,0:T(8,128)}, u32[]{:S(2)}) %copy-start.4) | copy-done | bytes 536
  6.2 0.0 copy-start.5
  6.2 32.6 %shard_map.101 = (f32[1024,128]{1,0:T(8,128)S(1)}, f32[1,128]{1,0:T(1,128)S(1)}) custom-call(bf16[128,4096]{1,0:T(8,128)(2,1)S(1)} %copy-done, bf16[128,4096]{1,0:T(8,128)(2,1)S(1)} %copy-done.1, bf16[128,4096]{1,0:T(8,128)(2,1)S(1)} %copy-done.2, bf16[128,4096]{1,0:T(8,128)(2,1)S(1)} %copy-done.3, f32[8,16]{1,0:T(8,128)S(1)} %copy-done.4), custom_call_target="tpu_custom_call" | custom-call | tf_op jit(solution)/shard_map/pallas_call | solution.py:219
  38.8 0.0 copy-done.5
  38.8 7.5 %shard_map.102 = (f32[128,4096]{1,0:T(8,128)}, f32[128,4096]{1,0:T(8,128)}, f32[128,4096]{1,0:T(8,128)}, f32[128,4096]{1,0:T(8,128)}, f32[8,16]{1,0:T(8,128)}) custom-call(bf16[128,4096]{1,0:T(8,128)(2,1)S(1)} %copy-done, bf16[128,4096]{1,0:T(8,128)(2,1)S(1)} %copy-done.1, bf16[128,4096]{1,0:T(8,128)(2,1)S(1)} %copy-done.2, bf16[128,4096]{1,0:T(8,128)(2,1)S(1)} %copy-done.3, ...), custom_call_target="tpu_custom_call" | custom-call | tf_op jit(solution)/shard_map/pallas_call | solution.py:319
Async XLA Ops:
  0.6 1.2 %copy-start = (bf16[128,4096]{1,0:T(8,128)(2,1)S(1)}, bf16[128,4096]{1,0:T(8,128)(2,1)}, u32[]{:S(2)}) copy-start(bf16[128,4096]{1,0:T(8,128)(2,1)} %refs_0_.3) | copy-start | bytes 3145732
  1.9 1.2 %copy-start.1 = (bf16[128,4096]{1,0:T(8,128)(2,1)S(1)}, bf16[128,4096]{1,0:T(8,128)(2,1)}, u32[]{:S(2)}) copy-start(bf16[128,4096]{1,0:T(8,128)(2,1)} %refs_1_.3) | copy-start | bytes 3145732
  3.1 1.2 %copy-start.2 = (bf16[128,4096]{1,0:T(8,128)(2,1)S(1)}, bf16[128,4096]{1,0:T(8,128)(2,1)}, u32[]{:S(2)}) copy-start(bf16[128,4096]{1,0:T(8,128)(2,1)} %refs_2_.3) | copy-start | bytes 3145732
  4.3 1.2 %copy-start.3 = (bf16[128,4096]{1,0:T(8,128)(2,1)S(1)}, bf16[128,4096]{1,0:T(8,128)(2,1)}, u32[]{:S(2)}) copy-start(bf16[128,4096]{1,0:T(8,128)(2,1)} %refs_3_.3) | copy-start | bytes 3145732
  5.5 0.7 %copy-start.4 = (f32[8,16]{1,0:T(8,128)S(1)}, f32[8,16]{1,0:T(8,128)}, u32[]{:S(2)}) copy-start(f32[8,16]{1,0:T(8,128)} %refs_7_.1) | copy-start | bytes 1540
  6.2 32.6 %copy-start.5 = (f32[8,16]{1,0:T(8,128)S(1)}, f32[8,16]{1,0:T(8,128)}, u32[]{:S(2)}) copy-start(f32[8,16]{1,0:T(8,128)} %refs_6_.1) | copy-start | bytes 1540

commit v2 on v1

v2 whole, which is shorter than its diff:
```python
import math

import jax
import jax.numpy as jnp
from jax import lax
from jax.experimental import pallas as pl
from jax.experimental.pallas import tpu as pltpu
from jax.sharding import PartitionSpec as P

GROUP = 512
MODES = 16
LANES = 128
TILE = 8
QUARTERS = GROUP // LANES
MESH = pl.DeviceIdType.MESH
MIB = 1024 * 1024


def iota(shape, axis):
    return lax.broadcasted_iota(jnp.int32, shape, axis)


def split(x):
    hi = x.astype(jnp.bfloat16)
    lo = (x - hi.astype(jnp.float32)).astype(jnp.bfloat16)
    return hi, lo


def dot(a, b):
    return jnp.dot(a, b, preferred_element_type=jnp.float32)


def column(row):
    eye = iota((MODES, MODES), 0) == iota((MODES, MODES), 1)
    return jnp.sum(jnp.where(eye, jnp.broadcast_to(row, (MODES, MODES)), 0.0), axis=1, keepdims=True)


def gated(a, b):
    return (a.astype(jnp.float32) * b.astype(jnp.float32)).astype(jnp.bfloat16)


def exchange_kernel(
    count, groups, span, inner,
    q_hbm, k_hbm, v_hbm, o_hbm, res_hbm, decay_hbm,
    state_ref, total_ref, ins, mixed_ref, conv_ref, rise_ref, fall_ref,
    prod, grad, send, theirs, comb, recv, back, half, sib, acol, xs, small,
    vbuf, v_one, v_two, v_three,
    load_sem, small_sem, swap_sem, sems,
):
    me = lax.axis_index("ctx") * inner + lax.axis_index("grp")
    chips = count // 2
    chip = lax.div(me, 2)
    core = lax.rem(me, 2)
    sibling = me + 1 - 2 * core
    part_groups = groups // 2
    part_rows = part_groups * MODES
    first = core * part_groups
    other = part_groups - first

    def place(j):
        return (lax.div(j, inner), lax.rem(j, inner))

    sources = (q_hbm, k_hbm, v_hbm, o_hbm)

    def load(g, n):
        return pltpu.make_async_copy(
            sources[n].at[:, pl.ds(pl.multiple_of(g * GROUP, GROUP), GROUP)],
            ins.at[n, g],
            load_sem.at[g, n],
        )

    tables = [
        pltpu.make_async_copy(decay_hbm, small.at[0], small_sem.at[0]),
        pltpu.make_async_copy(res_hbm, small.at[1], small_sem.at[1]),
    ]
    for copy in tables:
        copy.start()

    def ordered(s):
        return jnp.where(s < part_groups, other + s, first + s - part_groups)

    for s in range(groups):
        for n in range(4):
            load(ordered(s), n).start()

    barrier = pltpu.get_barrier_semaphore()
    pl.semaphore_signal(barrier, inc=1, device_id=place(sibling), device_id_type=MESH)

    def peer(d):
        return lax.rem(chip + d, chips)

    def greet(d, c):
        pl.semaphore_signal(
            barrier, inc=1, device_id=place(peer(d) * 2 + core), device_id_type=MESH
        )
        return c

    lax.fori_loop(1, chips, greet, 0)

    lane_i = iota((MODES, LANES), 1)
    lane = lane_i.astype(jnp.float32)
    for copy in tables:
        copy.wait()
    for g in range(groups):
        rates = jnp.broadcast_to(column(small[0, g : g + 1, :]), (MODES, LANES))
        acol[g * MODES : (g + 1) * MODES, :] = rates

    def group_rates(g):
        return acol[pl.ds(pl.multiple_of(g * MODES, MODES), MODES), :]

    block = MODES * TILE

    def swap_copy(source, target, n, where, phase):
        return pltpu.make_async_remote_copy(
            src_ref=source.at[pl.ds(pl.multiple_of(where, block), block), :],
            dst_ref=target.at[pl.ds(n * block, block), :],
            send_sem=swap_sem.at[phase, 0, n],
            recv_sem=swap_sem.at[phase, 1, n],
            device_id=place(sibling),
            device_id_type=MESH,
        )

    def out_copy(n):
        return swap_copy(send, theirs, n, (other + n) * block, 0)

    def states(s, c):
        g = ordered(s)
        for n in range(4):
            load(g, n).wait()
        p = gated(ins[1, g], ins[2, g])
        r = gated(ins[3, g], ins[0, g])
        prod[g] = p
        grad[g] = r
        rates = group_rates(g)
        to_end = jnp.concatenate(split(jnp.exp(-rates * (span - 1.0 - lane))), axis=0)
        from_start = jnp.concatenate(split(jnp.exp(-rates * lane)), axis=0)
        ends = dot(to_end, p)
        starts = dot(from_start, r)
        ends = ends[:MODES] + ends[MODES:]
        starts = starts[:MODES] + starts[MODES:]
        for k in range(QUARTERS):
            cut = slice(k * LANES, (k + 1) * LANES)
            send[pl.ds(g * block + k, MODES, stride=TILE), :] = ends[:, cut]
            send[pl.ds(g * block + QUARTERS + k, MODES, stride=TILE), :] = starts[:, cut]
        return c

    lax.fori_loop(0, part_groups, states, 0)
    pl.semaphore_wait(barrier, chips)
    for n in range(part_groups):
        out_copy(n).start()
    lax.fori_loop(part_groups, groups, states, 0)

    sub = iota((TILE, LANES), 0)
    lead = (sub < QUARTERS) == (core == 0)

    def row_factor(n, width):
        rate = acol[pl.ds(first * MODES + n, 1), :]
        return jnp.broadcast_to(jnp.exp(-rate * float(span)), (width, LANES))

    def tile_at(n):
        return pl.ds(pl.multiple_of(n * TILE, TILE), TILE)

    def own_tile(n):
        return pl.ds(pl.multiple_of(first * block + n * TILE, TILE), TILE)

    def combine(n, c):
        factor = row_factor(n, TILE)
        mine = send[own_tile(n), :]
        got = theirs[tile_at(n), :]
        comb[tile_at(n), :] = jnp.where(lead, factor, 1.0) * mine + jnp.where(lead, 1.0, factor) * got
        return c

    for n in range(part_groups):
        out_copy(n).wait_recv()
        lax.fori_loop(n * MODES, (n + 1) * MODES, combine, 0, unroll=8)

    def scatter(source, target, send_sem, recv_sem):
        def one(d, c):
            t = peer(d)
            pltpu.make_async_remote_copy(
                src_ref=source.at[tile_at(t), :],
                dst_ref=target.at[tile_at(chip), :],
                send_sem=send_sem,
                recv_sem=recv_sem,
                device_id=place(t * 2 + core),
                device_id_type=MESH,
            ).start()
            return c

        lax.fori_loop(1, chips, one, 0)

    def await_all(ref, sem):
        part = ref.at[pl.ds(0, (chips - 1) * TILE), :]
        pltpu.make_async_copy(part, part, sem).wait()

    scatter(comb, recv, sems.at[0], sems.at[1])

    row = iota((span, LANES), 0)
    col = iota((span, LANES), 1)
    flip = (row + col == span - 1).astype(jnp.bfloat16)
    here = lane_i - iota((MODES, LANES), 0)

    xs[...] = jnp.zeros_like(xs)

    def within_chip(n, c):
        base = pl.multiple_of(first * block + n * TILE, TILE)
        near = pl.multiple_of(n * TILE, TILE)
        early = jnp.where(
            core == 0,
            send[pl.ds(base, QUARTERS), :] * theirs[pl.ds(near + QUARTERS, QUARTERS), :],
            theirs[pl.ds(near, QUARTERS), :] * send[pl.ds(base + QUARTERS, QUARTERS), :],
        )
        xs[pl.ds(first * MODES + n, 1), :] = jnp.sum(early, axis=0, keepdims=True)
        return c

    lax.fori_loop(0, part_rows, within_chip, 0, unroll=8)

    def pairs(g, total):
        pair = lax.dot_general(
            prod[g], grad[g], (((1,), (1,)), ((), ())), preferred_element_type=jnp.float32
        )
        hi, lo = split(pair)
        turned = dot(hi, flip) + dot(lo, flip)
        lagged = pltpu.roll(turned, 0, 1, stride=1, stride_axis=0)
        cross = jnp.sum(jnp.where(col >= row, lagged, 0.0), axis=0, keepdims=True)
        rates = group_rates(g)
        chip_part = xs[pl.ds(pl.multiple_of(g * MODES, MODES), MODES), :]
        inside = jnp.exp(-rates * (span - 1.0 - lane)) * cross + jnp.exp(-rates) * chip_part
        inside = jnp.sum(inside, axis=1, keepdims=True)
        return total + jnp.sum(jnp.where(here == g * MODES, inside, 0.0), axis=0, keepdims=True)

    share = lax.fori_loop(0, groups, pairs, jnp.zeros((1, LANES), jnp.float32))

    turned_lags = jnp.where(lane_i == 0, 0, LANES - lane_i).astype(jnp.float32)
    triple = 3 * MODES
    token = iota((span, triple), 0).astype(jnp.float32)
    which = iota((span, triple), 1)

    def local(g, c):
        rates = group_rates(g)
        decay_row = small[0, pl.ds(g, 1), :]
        res_row = small[1, pl.ds(g, 1), :]
        weights = column(res_row)

        def toeplitz(lags, keep):
            line = jnp.sum(weights * jnp.exp(-rates * lags), axis=0, keepdims=True)
            full = pltpu.roll(jnp.broadcast_to(line, (span, LANES)), 0, 1, stride=1, stride_axis=0)
            return jnp.concatenate(split(jnp.where(keep, full, 0.0)), axis=1)

        p = prod[g]
        r = grad[g]
        mixed_ref[g] = dot(toeplitz(turned_lags, row >= col), jnp.concatenate([p, p], axis=0))
        conv_ref[g] = dot(toeplitz(lane, row <= col), jnp.concatenate([r, r], axis=0))
        decay_rows = jnp.concatenate([decay_row] * 3, axis=1)
        res_rows = jnp.concatenate([res_row] * 3, axis=1)

        def table(distance):
            hi, lo = split(res_rows * jnp.exp(-decay_rows * distance))
            return jnp.where(which < 2 * MODES, hi.astype(jnp.float32), lo.astype(jnp.float32)).astype(
                jnp.bfloat16
            )

        rise_ref[g] = table(token + 1.0)
        fall_ref[g] = table(span - token)
        return c

    lax.fori_loop(0, part_groups, local, 0)

    own = tile_at(chip)
    await_all(recv, sems.at[1])
    recv[own, :] = comb[own, :]

    rate = jnp.broadcast_to(acol[pl.ds(first * MODES + chip, 1), :], (QUARTERS, LANES))
    leap = jnp.exp(-rate * (2.0 * span))
    zero = jnp.zeros((QUARTERS, LANES), jnp.float32)

    def step(i, carry):
        rising, falling, acc = carry
        up = pl.multiple_of(i * TILE, TILE)
        down = pl.multiple_of((chips - 1 - i) * TILE, TILE)
        back[pl.ds(up, QUARTERS), :] = rising
        back[pl.ds(down + QUARTERS, QUARTERS), :] = falling
        acc = acc + rising * recv[pl.ds(up + QUARTERS, QUARTERS), :]
        rising = leap * rising + recv[pl.ds(up, QUARTERS), :]
        falling = leap * falling + recv[pl.ds(down + QUARTERS, QUARTERS), :]
        return rising, falling, acc

    rising, falling, acc = lax.fori_loop(0, chips, step, (zero, zero, zero), unroll=8)
    scatter(back, half, sems.at[2], sems.at[3])
    half[own, :] = back[own, :]

    total = jnp.sum(jnp.sum(jnp.exp(-rate) * acc, axis=0, keepdims=True), axis=1, keepdims=True)
    mode = iota((1, LANES), 1) == first * MODES + chip
    share = share + jnp.where(mode, jnp.broadcast_to(total, (1, LANES)), 0.0)

    def reduce(level, buf, radix, stride, value, begin, end):
        digit = lax.rem(lax.div(me, stride), radix)
        base = me - digit * stride
        send_sem = sems.at[4 + 2 * level]
        recv_sem = sems.at[5 + 2 * level]
        vbuf[level] = value
        for d in range(1, radix):
            pltpu.make_async_remote_copy(
                src_ref=vbuf.at[level],
                dst_ref=buf.at[digit],
                send_sem=send_sem,
                recv_sem=recv_sem,
                device_id=place(base + lax.rem(digit + d, radix) * stride),
                device_id_type=MESH,
            ).start()
        lax.fori_loop(begin, end, local, 0)
        part = buf.at[pl.ds(0, radix - 1)]
        pltpu.make_async_copy(part, part, recv_sem).wait()
        buf[digit] = value
        summed = jnp.sum(buf[...], axis=0)
        pltpu.make_async_copy(part, part, send_sem).wait()
        return summed

    share = reduce(0, v_one, 2, 1, share, part_groups, part_groups + 1)
    share = reduce(1, v_two, 8, 2, share, part_groups + 1, groups)
    share = reduce(2, v_three, 8, 16, share, 0, 0)
    total_ref[...] = share

    await_all(half, sems.at[3])

    def back_copy(n):
        return pltpu.make_async_remote_copy(
            src_ref=sib.at[pl.ds(n * block, block), :],
            dst_ref=state_ref.at[pl.ds(pl.multiple_of((first + n) * block, block), block), :],
            send_sem=swap_sem.at[1, 0, n],
            recv_sem=swap_sem.at[1, 1, n],
            device_id=place(sibling),
            device_id_type=MESH,
        )

    def for_sibling(n, c):
        x = half[tile_at(n), :]
        factor = row_factor(n, TILE)
        sib[tile_at(n), :] = jnp.where(lead, factor * x + send[own_tile(n), :], x)
        return c

    def for_me(n, c):
        x = half[tile_at(n), :]
        factor = row_factor(n, TILE)
        state_ref[own_tile(n), :] = jnp.where(lead, x, factor * x + theirs[tile_at(n), :])
        return c

    for n in range(part_groups):
        lax.fori_loop(n * MODES, (n + 1) * MODES, for_sibling, 0, unroll=8)
        back_copy(n).start()
    lax.fori_loop(0, part_rows, for_me, 0, unroll=8)

    for n in range(part_groups):
        out_copy(n).wait_send()
        back_copy(n).wait()
    await_all(comb, sems.at[0])
    await_all(back, sems.at[2])


def exchange(query_input, key_input, value_input, out_grad, residues, decays):
    inner = lax.axis_size("grp")
    count = lax.axis_size("ctx") * inner
    span, width = query_input.shape
    groups = width // GROUP
    rows = groups * MODES * TILE
    chips = count // 2
    f32 = jnp.float32
    bf16 = jnp.bfloat16

    def body(*refs):
        exchange_kernel(count, groups, span, inner, *refs)

    hbm = pl.BlockSpec(memory_space=pltpu.HBM)
    vmem = pl.BlockSpec(memory_space=pltpu.VMEM)
    return pl.pallas_call(
        body,
        out_shape=(
            jax.ShapeDtypeStruct((rows, LANES), f32),
            jax.ShapeDtypeStruct((1, LANES), f32),
            jax.ShapeDtypeStruct((4, groups, span, GROUP), bf16),
            jax.ShapeDtypeStruct((groups, span, GROUP), f32),
            jax.ShapeDtypeStruct((groups, span, GROUP), f32),
            jax.ShapeDtypeStruct((groups, span, 3 * MODES), bf16),
            jax.ShapeDtypeStruct((groups, span, 3 * MODES), bf16),
        ),
        in_specs=[hbm] * 6,
        out_specs=(vmem,) * 7,
        scratch_shapes=[
            pltpu.VMEM((groups, span, GROUP), bf16),
            pltpu.VMEM((groups, span, GROUP), bf16),
            pltpu.VMEM((rows, LANES), f32),
            pltpu.VMEM((rows // 2, LANES), f32),
            pltpu.VMEM((rows // 2, LANES), f32),
            pltpu.VMEM((chips * TILE, LANES), f32),
            pltpu.VMEM((chips * TILE, LANES), f32),
            pltpu.VMEM((rows // 2, LANES), f32),
            pltpu.VMEM((rows // 2, LANES), f32),
            pltpu.VMEM((groups * MODES, LANES), f32),
            pltpu.VMEM((groups * MODES, LANES), f32),
            pltpu.VMEM((2, groups, MODES), f32),
            pltpu.VMEM((3, 1, LANES), f32),
            pltpu.VMEM((2, 1, LANES), f32),
            pltpu.VMEM((8, 1, LANES), f32),
            pltpu.VMEM((8, 1, LANES), f32),
            pltpu.SemaphoreType.DMA((groups, 4)),
            pltpu.SemaphoreType.DMA((2,)),
            pltpu.SemaphoreType.DMA((2, 2, groups // 2)),
            pltpu.SemaphoreType.DMA((10,)),
        ],
        compiler_params=pltpu.CompilerParams(
            collective_id=0, has_side_effects=True, vmem_limit_bytes=20 * MIB
        ),
    )(
        *(
            pltpu.with_memory_space_constraint(a, pltpu.HBM)
            for a in (query_input, key_input, value_input, out_grad, residues, decays)
        )
    )


def finish_kernel(
    groups, scale,
    state_ref, total_ref, ins, mixed_ref, conv_ref, rise_ref, fall_ref,
    out_hbm, qg_hbm, kg_hbm, vg_hbm, rg_ref,
    outs, sems,
):
    targets = (out_hbm, qg_hbm, kg_hbm, vg_hbm)

    def store(g, n):
        return pltpu.make_async_copy(
            outs.at[n, g],
            targets[n].at[:, pl.ds(pl.multiple_of(g * GROUP, GROUP), GROUP)],
            sems.at[n, g],
        )

    def carried(table, g, offset):
        state = jnp.concatenate(
            [
                state_ref[pl.ds(g * MODES * TILE + offset + n, MODES, stride=TILE), :]
                for n in range(QUARTERS)
            ],
            axis=1,
        )
        hi, lo = split(state)
        return dot(table, jnp.concatenate([hi, lo, hi], axis=0))

    def one(g, c):
        mixed = mixed_ref[g] + carried(rise_ref[g], g, 0)
        outs[0, g] = ins[0, g].astype(jnp.float32) * mixed
        store(g, 0).start()
        outs[1, g] = ins[3, g].astype(jnp.float32) * mixed
        store(g, 1).start()
        conv = conv_ref[g] + carried(fall_ref[g], g, QUARTERS)
        outs[2, g] = ins[2, g].astype(jnp.float32) * conv
        store(g, 2).start()
        outs[3, g] = ins[1, g].astype(jnp.float32) * conv
        store(g, 3).start()
        return c

    lax.fori_loop(0, groups, one, 0)

    spread = jnp.broadcast_to(total_ref[...], (groups, LANES))
    own = lax.div(iota((groups, LANES), 1), MODES) == iota((groups, LANES), 0)
    spread = jnp.where(own, spread, 0.0)
    out = spread
    for n in range(1, groups):
        out = out + pltpu.roll(spread, LANES - n * MODES, 1)
    rg_ref[...] = out[:, :MODES] * scale

    for g in range(groups):
        for n in range(4):
            store(g, n).wait()


def finish(parts, span, width, length):
    groups = width // GROUP
    scale = 1.0 / (length * math.sqrt(GROUP))

    def body(*refs):
        finish_kernel(groups, scale, *refs)

    hbm = pl.BlockSpec(memory_space=pltpu.HBM)
    vmem = pl.BlockSpec(memory_space=pltpu.VMEM)
    big = jax.ShapeDtypeStruct((span, width), jnp.float32)
    return pl.pallas_call(
        body,
        out_shape=(big, big, big, big, jax.ShapeDtypeStruct((groups, MODES), jnp.float32)),
        in_specs=[vmem] * 7,
        out_specs=(hbm, hbm, hbm, hbm, vmem),
        scratch_shapes=[
            pltpu.VMEM((4, groups, span, GROUP), jnp.float32),
            pltpu.SemaphoreType.DMA((4, groups)),
        ],
        compiler_params=pltpu.CompilerParams(vmem_limit_bytes=20 * MIB),
    )(*parts)


def on_device(query_input, key_input, value_input, out_grad, residues, decay_rates):
    span, width = query_input.shape
    length = span * lax.axis_size("ctx") * lax.axis_size("grp")
    parts = exchange(query_input, key_input, value_input, out_grad, residues, decay_rates)
    return finish(parts, span, width, length)


def solution(mesh):
    rows = P(("ctx", "grp"), None)
    return jax.shard_map(
        on_device,
        mesh=mesh,
        in_specs=(rows, rows, rows, rows, P(), P()),
        out_specs=(rows, rows, rows, rows, P()),
        check_vma=False,
    )
```

time: 46.9 us -> 37.1 us (0.79); the launches traced: 46.3 us -> 37 us
  local copies, waits for them, and re-layouts: 5.58 us -> 0 us
  Pallas kernels: 40 us -> 36.4 us
    unnamed x12 -> x0, local copies, waits for them, and re-layouts: 5.58 us -> none
    pallas_call x1, Pallas kernels: 7.45 us -> 4.33 us  [finish(): pl.pallas_call(body, out_shape=(big, big, big, big, jax.ShapeDtypeStruct(...]
    pallas_call x1, Pallas kernels: 32.6 us -> 32 us  [exchange(): pl.pallas_call(body, out_shape=(jax.ShapeDtypeStruct((rows, LANES), f32),...]
where the time goes in v2:
time: 37.1 us; the launch traced here: 37 us
  Pallas kernels  36.4 us (98%)
  between operations  0.64 us (2%)
    pallas_call x1, Pallas kernels, exchange(): pl.pallas_call(body, out_shape=(jax.ShapeDtypeStruct((rows, LANES), f32),...  32 us
    pallas_call x1, Pallas kernels, finish(): pl.pallas_call(body, out_shape=(big, big, big, big, jax.ShapeDtypeStruct(...  4.33 us

profile of v2, /device:TPU:1, one launch (start us, length us, event | category | flops | bytes accessed | tf_op | source)
XLA Modules:
  0.0 37.0 jit_solution(10225835987102958184)
XLA Ops:
  0.6 32.0 %shard_map.101 = (f32[1024,128]{1,0:T(8,128)S(1)}, f32[1,128]{1,0:T(1,128)S(1)}, bf16[4,8,128,512]{3,2,1,0:T(8,128)(2,1)S(1)}, f32[8,128,512]{2,1,0:T(8,128)S(1)...) custom-call(bf16[128,4096]{1,0:T(8,128)(2,1)} %refs_0_.1, ...), custom_call_target="tpu_custom_call" | custom-call | tf_op jit(solution)/shard_map/pallas_call | solution.py:375
  32.7 4.3 %shard_map.102 = (f32[128,4096]{1,0:T(8,128)}, f32[128,4096]{1,0:T(8,128)}, f32[128,4096]{1,0:T(8,128)}, f32[128,4096]{1,0:T(8,128)}, f32[8,16]{1,0:T(8,128)}) custom-call(f32[1024,128]{1,0:T(8,128)S(1)} %get-tuple-element.12.refs_0_, f32[1,128]{1,0:T(1,128)S(1)} %get-tuple-element.13.refs_1_, bf16[4,8,128,512]{3,2,1,0:T(8,128)(2,1)S(1)} %get-tuple-element.14.refs_2_, ...), custom_call_target="tpu_custom_call" | custom-call | tf_op jit(solution)/shard_map/pallas_call | solution.py:485

commit v3 on v2

--- a/solution.py
+++ b/solution.py
@@ -12,6 +12,8 @@
 LANES = 128
 TILE = 8
 QUARTERS = GROUP // LANES
+RING = 4
+EXTRA = TILE + 1
 MESH = pl.DeviceIdType.MESH
 MIB = 1024 * 1024
 
@@ -37,6 +39,12 @@
 
 def gated(a, b):
     return (a.astype(jnp.float32) * b.astype(jnp.float32)).astype(jnp.bfloat16)
+
+
+def shifts():
+    hops = (0, 1, 2, 1)
+    every = [(z, y, x) for z in range(RING) for y in range(RING) for x in range(RING)]
+    return sorted(every[1:], key=lambda d: -sum(hops[c] for c in d))
 
 
 def exchange_kernel(
@@ -44,7 +52,7 @@
     q_hbm, k_hbm, v_hbm, o_hbm, res_hbm, decay_hbm,
     state_ref, total_ref, ins, mixed_ref, conv_ref, rise_ref, fall_ref,
     prod, grad, send, theirs, comb, recv, back, half, sib, acol, xs, small,
-    vbuf, v_one, v_two, v_three,
+    vbuf, v_one, v_two, v_got,
     load_sem, small_sem, swap_sem, sems,
 ):
     me = lax.axis_index("ctx") * inner + lax.axis_index("grp")
@@ -69,6 +77,28 @@
             load_sem.at[g, n],
         )
 
+    def ordered(s):
+        return jnp.where(s < part_groups, other + s, first + s - part_groups)
+
+    barrier = pltpu.get_barrier_semaphore()
+    pl.semaphore_signal(barrier, inc=1, device_id=place(sibling), device_id_type=MESH)
+
+    y_hi = lax.rem(chip, 2)
+    x = lax.rem(lax.div(chip, 2), RING)
+    y = y_hi * 2 + lax.rem(lax.div(chip, 2 * RING), 2)
+    z = lax.div(chip, 4 * RING)
+
+    def peer(d):
+        dz, dy, dx = d
+        to_z, to_y, to_x = lax.rem(z + dz, RING), lax.rem(y + dy, RING), lax.rem(x + dx, RING)
+        return ((to_z * 2 + lax.rem(to_y, 2)) * RING + to_x) * 2 + lax.div(to_y, 2)
+
+    peers = [peer(d) for d in shifts()]
+    for t in peers:
+        pl.semaphore_signal(
+            barrier, inc=1, device_id=place(t * 2 + core), device_id_type=MESH
+        )
+
     tables = [
         pltpu.make_async_copy(decay_hbm, small.at[0], small_sem.at[0]),
         pltpu.make_async_copy(res_hbm, small.at[1], small_sem.at[1]),
@@ -76,26 +106,9 @@
     for copy in tables:
         copy.start()
 
-    def ordered(s):
-        return jnp.where(s < part_groups, other + s, first + s - part_groups)
-
     for s in range(groups):
         for n in range(4):
             load(ordered(s), n).start()
-
-    barrier = pltpu.get_barrier_semaphore()
-    pl.semaphore_signal(barrier, inc=1, device_id=place(sibling), device_id_type=MESH)
-
-    def peer(d):
-        return lax.rem(chip + d, chips)
-
-    def greet(d, c):
-        pl.semaphore_signal(
-            barrier, inc=1, device_id=place(peer(d) * 2 + core), device_id_type=MESH
-        )
-        return c
-
-    lax.fori_loop(1, chips, greet, 0)
 
     lane_i = iota((MODES, LANES), 1)
     lane = lane_i.astype(jnp.float32)
@@ -175,25 +188,22 @@
         lax.fori_loop(n * MODES, (n + 1) * MODES, combine, 0, unroll=8)
 
     def scatter(source, target, send_sem, recv_sem):
-        def one(d, c):
-            t = peer(d)
+        for t in peers:
             pltpu.make_async_remote_copy(
-                src_ref=source.at[tile_at(t), :],
-                dst_ref=target.at[tile_at(chip), :],
+                src_ref=source(t),
+                dst_ref=target(chip),
                 send_sem=send_sem,
                 recv_sem=recv_sem,
                 device_id=place(t * 2 + core),
                 device_id_type=MESH,
             ).start()
-            return c
-
-        lax.fori_loop(1, chips, one, 0)
-
-    def await_all(ref, sem):
-        part = ref.at[pl.ds(0, (chips - 1) * TILE), :]
+
+    def await_all(part, sem):
         pltpu.make_async_copy(part, part, sem).wait()
 
-    scatter(comb, recv, sems.at[0], sems.at[1])
+    most = pl.ds(0, (chips - 1) * TILE)
+    rest = pl.ds(0, chips - 1)
+    scatter(lambda t: comb.at[tile_at(t), :], lambda t: recv.at[tile_at(t), :], sems.at[0], sems.at[1])
 
     row = iota((span, LANES), 0)
     col = iota((span, LANES), 1)
@@ -231,6 +241,31 @@
 
     share = lax.fori_loop(0, groups, pairs, jnp.zeros((1, LANES), jnp.float32))
 
+    def reduce_start(level, buf, radix, stride, value):
+        digit = lax.rem(lax.div(chip, stride), radix)
+        base = chip - digit * stride
+        vbuf[level] = value
+        buf[digit] = value
+        for d in range(1, radix):
+            pltpu.make_async_remote_copy(
+                src_ref=vbuf.at[level],
+                dst_ref=buf.at[digit],
+                send_sem=sems.at[4 + 2 * level],
+                recv_sem=sems.at[5 + 2 * level],
+                device_id=place((base + lax.rem(digit + d, radix) * stride) * 2 + core),
+                device_id_type=MESH,
+            ).start()
+
+    def reduce_end(level, buf, radix):
+        part = buf.at[pl.ds(0, radix - 1)]
+        await_all(part, sems.at[5 + 2 * level])
+        await_all(part, sems.at[4 + 2 * level])
+        return jnp.sum(buf[...], axis=0)
+
+    radix_one = 2 * RING
+    radix_two = chips // radix_one
+    reduce_start(0, v_one, radix_one, 1, share)
+
     turned_lags = jnp.where(lane_i == 0, 0, LANES - lane_i).astype(jnp.float32)
     triple = 3 * MODES
     token = iota((span, triple), 0).astype(jnp.float32)
@@ -267,7 +302,7 @@
     lax.fori_loop(0, part_groups, local, 0)
 
     own = tile_at(chip)
-    await_all(recv, sems.at[1])
+    await_all(recv.at[most, :], sems.at[1])
     recv[own, :] = comb[own, :]
 
     rate = jnp.broadcast_to(acol[pl.ds(first * MODES + chip, 1), :], (QUARTERS, LANES))
@@ -278,50 +313,25 @@
         rising, falling, acc = carry
         up = pl.multiple_of(i * TILE, TILE)
         down = pl.multiple_of((chips - 1 - i) * TILE, TILE)
-        back[pl.ds(up, QUARTERS), :] = rising
-        back[pl.ds(down + QUARTERS, QUARTERS), :] = falling
+        back[i, pl.ds(0, QUARTERS), :] = rising
+        back[chips - 1 - i, pl.ds(QUARTERS, QUARTERS), :] = falling
         acc = acc + rising * recv[pl.ds(up + QUARTERS, QUARTERS), :]
         rising = leap * rising + recv[pl.ds(up, QUARTERS), :]
         falling = leap * falling + recv[pl.ds(down + QUARTERS, QUARTERS), :]
         return rising, falling, acc
 
     rising, falling, acc = lax.fori_loop(0, chips, step, (zero, zero, zero), unroll=8)
-    scatter(back, half, sems.at[2], sems.at[3])
-    half[own, :] = back[own, :]
-
-    total = jnp.sum(jnp.sum(jnp.exp(-rate) * acc, axis=0, keepdims=True), axis=1, keepdims=True)
-    mode = iota((1, LANES), 1) == first * MODES + chip
-    share = share + jnp.where(mode, jnp.broadcast_to(total, (1, LANES)), 0.0)
-
-    def reduce(level, buf, radix, stride, value, begin, end):
-        digit = lax.rem(lax.div(me, stride), radix)
-        base = me - digit * stride
-        send_sem = sems.at[4 + 2 * level]
-        recv_sem = sems.at[5 + 2 * level]
-        vbuf[level] = value
-        for d in range(1, radix):
-            pltpu.make_async_remote_copy(
-                src_ref=vbuf.at[level],
-                dst_ref=buf.at[digit],
-                send_sem=send_sem,
-                recv_sem=recv_sem,
-                device_id=place(base + lax.rem(digit + d, radix) * stride),
-                device_id_type=MESH,
-            ).start()
-        lax.fori_loop(begin, end, local, 0)
-        part = buf.at[pl.ds(0, radix - 1)]
-        pltpu.make_async_copy(part, part, recv_sem).wait()
-        buf[digit] = value
-        summed = jnp.sum(buf[...], axis=0)
-        pltpu.make_async_copy(part, part, send_sem).wait()
-        return summed
-
-    share = reduce(0, v_one, 2, 1, share, part_groups, part_groups + 1)
-    share = reduce(1, v_two, 8, 2, share, part_groups + 1, groups)
-    share = reduce(2, v_three, 8, 16, share, 0, 0)
-    total_ref[...] = share
-
-    await_all(half, sems.at[3])
+    pooled = jnp.sum(jnp.exp(-rate) * acc, axis=0, keepdims=True)
+    for t in range(chips):
+        back[t, TILE : TILE + 1, :] = pooled
+    scatter(lambda t: back.at[t], lambda t: half.at[t], sems.at[2], sems.at[3])
+    half[chip] = back[chip]
+
+    share = reduce_end(0, v_one, radix_one)
+    reduce_start(1, v_two, radix_two, radix_one, share)
+    lax.fori_loop(part_groups, groups, local, 0)
+
+    await_all(half.at[rest], sems.at[3])
 
     def back_copy(n):
         return pltpu.make_async_remote_copy(
@@ -334,13 +344,13 @@
         )
 
     def for_sibling(n, c):
-        x = half[tile_at(n), :]
+        x = half[n, pl.ds(0, TILE), :]
         factor = row_factor(n, TILE)
         sib[tile_at(n), :] = jnp.where(lead, factor * x + send[own_tile(n), :], x)
         return c
 
     def for_me(n, c):
-        x = half[tile_at(n), :]
+        x = half[n, pl.ds(0, TILE), :]
         factor = row_factor(n, TILE)
         state_ref[own_tile(n), :] = jnp.where(lead, x, factor * x + theirs[tile_at(n), :])
         return c
@@ -348,13 +358,30 @@
     for n in range(part_groups):
         lax.fori_loop(n * MODES, (n + 1) * MODES, for_sibling, 0, unroll=8)
         back_copy(n).start()
+    share = reduce_end(1, v_two, radix_two)
+    pools = jnp.concatenate([half[t, TILE : TILE + 1, :] for t in range(chips)], axis=0)
+    pools = jnp.sum(pools, axis=1, keepdims=True)
+    spot = iota((chips, LANES), 1) - iota((chips, LANES), 0) == first * MODES
+    share = share + jnp.sum(jnp.where(spot, pools, 0.0), axis=0, keepdims=True)
+    vbuf[2] = share
+    last = pltpu.make_async_remote_copy(
+        src_ref=vbuf.at[2],
+        dst_ref=v_got.at[0],
+        send_sem=sems.at[8],
+        recv_sem=sems.at[9],
+        device_id=place(sibling),
+        device_id_type=MESH,
+    )
+    last.start()
     lax.fori_loop(0, part_rows, for_me, 0, unroll=8)
+    last.wait()
+    total_ref[...] = share + v_got[0]
 
     for n in range(part_groups):
         out_copy(n).wait_send()
         back_copy(n).wait()
-    await_all(comb, sems.at[0])
-    await_all(back, sems.at[2])
+    await_all(comb.at[most, :], sems.at[0])
+    await_all(back.at[rest], sems.at[2])
 
 
 def exchange(query_input, key_input, value_input, out_grad, residues, decays):
@@ -392,16 +419,16 @@
             pltpu.VMEM((rows // 2, LANES), f32),
             pltpu.VMEM((rows // 2, LANES), f32),
             pltpu.VMEM((chips * TILE, LANES), f32),
-            pltpu.VMEM((chips * TILE, LANES), f32),
-            pltpu.VMEM((rows // 2, LANES), f32),
+            pltpu.VMEM((chips, EXTRA, LANES), f32),
+            pltpu.VMEM((chips, EXTRA, LANES), f32),
             pltpu.VMEM((rows // 2, LANES), f32),
             pltpu.VMEM((groups * MODES, LANES), f32),
             pltpu.VMEM((groups * MODES, LANES), f32),
             pltpu.VMEM((2, groups, MODES), f32),
             pltpu.VMEM((3, 1, LANES), f32),
-            pltpu.VMEM((2, 1, LANES), f32),
-            pltpu.VMEM((8, 1, LANES), f32),
-            pltpu.VMEM((8, 1, LANES), f32),
+            pltpu.VMEM((2 * RING, 1, LANES), f32),
+            pltpu.VMEM((chips // (2 * RING), 1, LANES), f32),
+            pltpu.VMEM((1, 1, LANES), f32),
             pltpu.SemaphoreType.DMA((groups, 4)),
             pltpu.SemaphoreType.DMA((2,)),
             pltpu.SemaphoreType.DMA((2, 2, groups // 2)),

time: 37.1 us -> 32.8 us (0.88)
  Pallas kernels: 36.4 us -> 32 us
    pallas_call x1, Pallas kernels: 32 us -> 27.7 us  [exchange(): pl.pallas_call(body, out_shape=(jax.ShapeDtypeStruct((rows, LANES), f32),...]
where the time goes in v3:
time: 32.8 us; the launch traced here: 32.7 us
  Pallas kernels  32 us (98%)
  between operations  0.64 us (2%)
    pallas_call x1, Pallas kernels, exchange(): pl.pallas_call(body, out_shape=(jax.ShapeDtypeStruct((rows, LANES), f32),...  27.7 us
    pallas_call x1, Pallas kernels, finish(): pl.pallas_call(body, out_shape=(big, big, big, big, jax.ShapeDtypeStruct(...  4.33 us

profile of v3, /device:TPU:1, one launch (start us, length us, event | category | flops | bytes accessed | tf_op | source)
XLA Modules:
  0.0 32.7 jit_solution(217374177523979811)
XLA Ops:
  0.6 27.7 %shard_map.101 = (f32[1024,128]{1,0:T(8,128)S(1)}, f32[1,128]{1,0:T(1,128)S(1)}, bf16[4,8,128,512]{3,2,1,0:T(8,128)(2,1)S(1)}, f32[8,128,512]{2,1,0:T(8,128)S(1)...) custom-call(bf16[128,4096]{1,0:T(8,128)(2,1)} %refs_0_.1, ...), custom_call_target="tpu_custom_call" | custom-call | tf_op jit(solution)/shard_map/pallas_call | solution.py:402
  28.3 4.3 %shard_map.102 = (f32[128,4096]{1,0:T(8,128)}, f32[128,4096]{1,0:T(8,128)}, f32[128,4096]{1,0:T(8,128)}, f32[128,4096]{1,0:T(8,128)}, f32[8,16]{1,0:T(8,128)}) custom-call(f32[1024,128]{1,0:T(8,128)S(1)} %get-tuple-element.12.refs_0_, f32[1,128]{1,0:T(1,128)S(1)} %get-tuple-element.13.refs_1_, bf16[4,8,128,512]{3,2,1,0:T(8,128)(2,1)S(1)} %get-tuple-element.14.refs_2_, ...), custom_call_target="tpu_custom_call" | custom-call | tf_op jit(solution)/shard_map/pallas_call | solution.py:512

commit v4 on v3

--- a/solution.py
+++ b/solution.py
@@ -41,6 +41,10 @@
     return (a.astype(jnp.float32) * b.astype(jnp.float32)).astype(jnp.bfloat16)
 
 
+FAR_PLANES = (2, 1, 3, 0)
+NEAR_PLANES = (0, 1, 3, 2)
+
+
 def shifts():
     hops = (0, 1, 2, 1)
     every = [(z, y, x) for z in range(RING) for y in range(RING) for x in range(RING)]
@@ -53,7 +57,7 @@
     state_ref, total_ref, ins, mixed_ref, conv_ref, rise_ref, fall_ref,
     prod, grad, send, theirs, comb, recv, back, half, sib, acol, xs, small,
     vbuf, v_one, v_two, v_got,
-    load_sem, small_sem, swap_sem, sems,
+    load_sem, small_sem, swap_sem, plane_sem, sems,
 ):
     me = lax.axis_index("ctx") * inner + lax.axis_index("grp")
     chips = count // 2
@@ -80,6 +84,7 @@
     def ordered(s):
         return jnp.where(s < part_groups, other + s, first + s - part_groups)
 
+
     barrier = pltpu.get_barrier_semaphore()
     pl.semaphore_signal(barrier, inc=1, device_id=place(sibling), device_id_type=MESH)
 
@@ -93,8 +98,8 @@
         to_z, to_y, to_x = lax.rem(z + dz, RING), lax.rem(y + dy, RING), lax.rem(x + dx, RING)
         return ((to_z * 2 + lax.rem(to_y, 2)) * RING + to_x) * 2 + lax.div(to_y, 2)
 
-    peers = [peer(d) for d in shifts()]
-    for t in peers:
+    peers = [(d, peer(d)) for d in shifts()]
+    for _, t in peers:
         pl.semaphore_signal(
             barrier, inc=1, device_id=place(t * 2 + core), device_id_type=MESH
         )
@@ -126,12 +131,15 @@
     def swap_copy(source, target, n, where, phase):
         return pltpu.make_async_remote_copy(
             src_ref=source.at[pl.ds(pl.multiple_of(where, block), block), :],
-            dst_ref=target.at[pl.ds(n * block, block), :],
+            dst_ref=target.at[pl.ds(pl.multiple_of(n * block, block), block), :],
             send_sem=swap_sem.at[phase, 0, n],
             recv_sem=swap_sem.at[phase, 1, n],
             device_id=place(sibling),
             device_id_type=MESH,
         )
+
+    def plane(d):
+        return lax.rem(z + d, RING)
 
     def out_copy(n):
         return swap_copy(send, theirs, n, (other + n) * block, 0)
@@ -157,11 +165,10 @@
             send[pl.ds(g * block + QUARTERS + k, MODES, stride=TILE), :] = starts[:, cut]
         return c
 
-    lax.fori_loop(0, part_groups, states, 0)
+    lax.fori_loop(0, groups, states, 0)
     pl.semaphore_wait(barrier, chips)
-    for n in range(part_groups):
-        out_copy(n).start()
-    lax.fori_loop(part_groups, groups, states, 0)
+    for d in FAR_PLANES:
+        out_copy(plane(d)).start()
 
     sub = iota((TILE, LANES), 0)
     lead = (sub < QUARTERS) == (core == 0)
@@ -169,6 +176,10 @@
     def row_factor(n, width):
         rate = acol[pl.ds(first * MODES + n, 1), :]
         return jnp.broadcast_to(jnp.exp(-rate * float(span)), (width, LANES))
+
+    def sweep(n, one):
+        for m in range(MODES):
+            one(n * MODES + m, 0)
 
     def tile_at(n):
         return pl.ds(pl.multiple_of(n * TILE, TILE), TILE)
@@ -183,27 +194,30 @@
         comb[tile_at(n), :] = jnp.where(lead, factor, 1.0) * mine + jnp.where(lead, 1.0, factor) * got
         return c
 
-    for n in range(part_groups):
-        out_copy(n).wait_recv()
-        lax.fori_loop(n * MODES, (n + 1) * MODES, combine, 0, unroll=8)
-
-    def scatter(source, target, send_sem, recv_sem):
-        for t in peers:
-            pltpu.make_async_remote_copy(
-                src_ref=source(t),
-                dst_ref=target(chip),
-                send_sem=send_sem,
-                recv_sem=recv_sem,
-                device_id=place(t * 2 + core),
-                device_id_type=MESH,
-            ).start()
+    def message(source, target, t, send_sem, recv_sem):
+        return pltpu.make_async_remote_copy(
+            src_ref=source,
+            dst_ref=target,
+            send_sem=send_sem,
+            recv_sem=recv_sem,
+            device_id=place(t * 2 + core),
+            device_id_type=MESH,
+        )
 
     def await_all(part, sem):
         pltpu.make_async_copy(part, part, sem).wait()
 
     most = pl.ds(0, (chips - 1) * TILE)
     rest = pl.ds(0, chips - 1)
-    scatter(lambda t: comb.at[tile_at(t), :], lambda t: recv.at[tile_at(t), :], sems.at[0], sems.at[1])
+    for d in FAR_PLANES:
+        n = plane(d)
+        out_copy(n).wait_recv()
+        sweep(n, combine)
+        for shift, t in peers:
+            if shift[0] == d:
+                message(
+                    comb.at[tile_at(t), :], recv.at[tile_at(chip), :], t, sems.at[0], sems.at[1]
+                ).start()
 
     row = iota((span, LANES), 0)
     col = iota((span, LANES), 1)
@@ -324,18 +338,17 @@
     pooled = jnp.sum(jnp.exp(-rate) * acc, axis=0, keepdims=True)
     for t in range(chips):
         back[t, TILE : TILE + 1, :] = pooled
-    scatter(lambda t: back.at[t], lambda t: half.at[t], sems.at[2], sems.at[3])
+    for _, t in peers:
+        message(back.at[t], half.at[chip], t, sems.at[2], plane_sem.at[z]).start()
     half[chip] = back[chip]
 
     share = reduce_end(0, v_one, radix_one)
     reduce_start(1, v_two, radix_two, radix_one, share)
     lax.fori_loop(part_groups, groups, local, 0)
 
-    await_all(half.at[rest], sems.at[3])
-
     def back_copy(n):
         return pltpu.make_async_remote_copy(
-            src_ref=sib.at[pl.ds(n * block, block), :],
+            src_ref=sib.at[pl.ds(pl.multiple_of(n * block, block), block), :],
             dst_ref=state_ref.at[pl.ds(pl.multiple_of((first + n) * block, block), block), :],
             send_sem=swap_sem.at[1, 0, n],
             recv_sem=swap_sem.at[1, 1, n],
@@ -355,14 +368,25 @@
         state_ref[own_tile(n), :] = jnp.where(lead, x, factor * x + theirs[tile_at(n), :])
         return c
 
-    for n in range(part_groups):
-        lax.fori_loop(n * MODES, (n + 1) * MODES, for_sibling, 0, unroll=8)
+    sum_rows = here - first * MODES
+    pooled_share = jnp.zeros((1, LANES), jnp.float32)
+    for d in NEAR_PLANES:
+        n = plane(d)
+        count_in = MODES - 1 if d == 0 else MODES
+        await_all(half.at[pl.ds(0, count_in)], plane_sem.at[n])
+        sweep(n, for_sibling)
         back_copy(n).start()
-    share = reduce_end(1, v_two, radix_two)
-    pools = jnp.concatenate([half[t, TILE : TILE + 1, :] for t in range(chips)], axis=0)
-    pools = jnp.sum(pools, axis=1, keepdims=True)
-    spot = iota((chips, LANES), 1) - iota((chips, LANES), 0) == first * MODES
-    share = share + jnp.sum(jnp.where(spot, pools, 0.0), axis=0, keepdims=True)
+        pools = jnp.concatenate(
+            [half[n * MODES + m, TILE : TILE + 1, :] for m in range(MODES)], axis=0
+        )
+        pools = jnp.sum(pools, axis=1, keepdims=True)
+        pooled_share = pooled_share + jnp.sum(
+            jnp.where(sum_rows == n * MODES, pools, 0.0), axis=0, keepdims=True
+        )
+        if d != NEAR_PLANES[-1]:
+            sweep(n, for_me)
+
+    share = reduce_end(1, v_two, radix_two) + pooled_share
     vbuf[2] = share
     last = pltpu.make_async_remote_copy(
         src_ref=vbuf.at[2],
@@ -373,7 +397,8 @@
         device_id_type=MESH,
     )
     last.start()
-    lax.fori_loop(0, part_rows, for_me, 0, unroll=8)
+    n = plane(NEAR_PLANES[-1])
+    sweep(n, for_me)
     last.wait()
     total_ref[...] = share + v_got[0]
 
@@ -432,6 +457,7 @@
             pltpu.SemaphoreType.DMA((groups, 4)),
             pltpu.SemaphoreType.DMA((2,)),
             pltpu.SemaphoreType.DMA((2, 2, groups // 2)),
+            pltpu.SemaphoreType.DMA((RING,)),
             pltpu.SemaphoreType.DMA((10,)),
         ],
         compiler_params=pltpu.CompilerParams(
@@ -448,8 +474,8 @@
 def finish_kernel(
     groups, scale,
     state_ref, total_ref, ins, mixed_ref, conv_ref, rise_ref, fall_ref,
-    out_hbm, qg_hbm, kg_hbm, vg_hbm, rg_ref,
-    outs, sems,
+    out_hbm, qg_hbm, kg_hbm, vg_hbm, rg_hbm,
+    outs, rg_ref, sems, rg_sem,
 ):
     targets = (out_hbm, qg_hbm, kg_hbm, vg_hbm)
 
@@ -493,10 +519,13 @@
     for n in range(1, groups):
         out = out + pltpu.roll(spread, LANES - n * MODES, 1)
     rg_ref[...] = out[:, :MODES] * scale
+    small = pltpu.make_async_copy(rg_ref, rg_hbm, rg_sem)
+    small.start()
 
     for g in range(groups):
         for n in range(4):
             store(g, n).wait()
+    small.wait()
 
 
 def finish(parts, span, width, length):
@@ -513,10 +542,12 @@
         body,
         out_shape=(big, big, big, big, jax.ShapeDtypeStruct((groups, MODES), jnp.float32)),
         in_specs=[vmem] * 7,
-        out_specs=(hbm, hbm, hbm, hbm, vmem),
+        out_specs=(hbm,) * 5,
         scratch_shapes=[
             pltpu.VMEM((4, groups, span, GROUP), jnp.float32),
+            pltpu.VMEM((groups, MODES), jnp.float32),
             pltpu.SemaphoreType.DMA((4, groups)),
+            pltpu.SemaphoreType.DMA(()),
         ],
         compiler_params=pltpu.CompilerParams(vmem_limit_bytes=20 * MIB),
     )(*parts)

time: 32.8 us -> 31.7 us (0.966)
  Pallas kernels: 32 us -> 30.9 us
    pallas_call x1, Pallas kernels: 4.33 us -> 3.75 us  [finish(): pl.pallas_call(body, out_shape=(big, big, big, big, jax.ShapeDtypeStruct(...]
    pallas_call x1, Pallas kernels: 27.7 us -> 27.2 us  [exchange(): pl.pallas_call(body, out_shape=(jax.ShapeDtypeStruct((rows, LANES), f32),...]
where the time goes in v4:
time: 31.7 us; the launch traced here: 31.6 us
  Pallas kernels  30.9 us (97%)
  between operations  0.64 us (2%)
    pallas_call x1, Pallas kernels, exchange(): pl.pallas_call(body, out_shape=(jax.ShapeDtypeStruct((rows, LANES), f32),...  27.2 us
    pallas_call x1, Pallas kernels, finish(): pl.pallas_call(body, out_shape=(big, big, big, big, jax.ShapeDtypeStruct(...  3.75 us

profile of v4, /device:TPU:1, one launch (start us, length us, event | category | flops | bytes accessed | tf_op | source)
XLA Modules:
  0.0 31.6 jit_solution(4250169201264004550)
XLA Ops:
  0.6 27.2 %shard_map.101 = (f32[1024,128]{1,0:T(8,128)S(1)}, f32[1,128]{1,0:T(1,128)S(1)}, bf16[4,8,128,512]{3,2,1,0:T(8,128)(2,1)S(1)}, f32[8,128,512]{2,1,0:T(8,128)S(1)...) custom-call(bf16[128,4096]{1,0:T(8,128)(2,1)} %refs_0_.1, ...), custom_call_target="tpu_custom_call" | custom-call | tf_op jit(solution)/shard_map/pallas_call | solution.py:427
  27.8 3.7 %shard_map.102 = (f32[128,4096]{1,0:T(8,128)}, f32[128,4096]{1,0:T(8,128)}, f32[128,4096]{1,0:T(8,128)}, f32[128,4096]{1,0:T(8,128)}, f32[8,16]{1,0:T(8,128)}) custom-call(f32[1024,128]{1,0:T(8,128)S(1)} %get-tuple-element.12.refs_0_, f32[1,128]{1,0:T(1,128)S(1)} %get-tuple-element.13.refs_1_, bf16[4,8,128,512]{3,2,1,0:T(8,128)(2,1)S(1)} %get-tuple-element.14.refs_2_, ...), custom_call_target="tpu_custom_call" | custom-call | tf_op jit(solution)/shard_map/pallas_call | solution.py:541

commit v5 on v4

--- a/solution.py
+++ b/solution.py
@@ -165,7 +165,8 @@
             send[pl.ds(g * block + QUARTERS + k, MODES, stride=TILE), :] = starts[:, cut]
         return c
 
-    lax.fori_loop(0, groups, states, 0)
+    for s in range(groups):
+        states(s, 0)
     pl.semaphore_wait(barrier, chips)
     for d in FAR_PLANES:
         out_copy(plane(d)).start()
@@ -253,7 +254,7 @@
         inside = jnp.sum(inside, axis=1, keepdims=True)
         return total + jnp.sum(jnp.where(here == g * MODES, inside, 0.0), axis=0, keepdims=True)
 
-    share = lax.fori_loop(0, groups, pairs, jnp.zeros((1, LANES), jnp.float32))
+    share = lax.fori_loop(0, groups, pairs, jnp.zeros((1, LANES), jnp.float32), unroll=4)
 
     def reduce_start(level, buf, radix, stride, value):
         digit = lax.rem(lax.div(chip, stride), radix)
@@ -313,7 +314,7 @@
         fall_ref[g] = table(span - token)
         return c
 
-    lax.fori_loop(0, part_groups, local, 0)
+    lax.fori_loop(0, part_groups, local, 0, unroll=2)
 
     own = tile_at(chip)
     await_all(recv.at[most, :], sems.at[1])
@@ -344,7 +345,7 @@
 
     share = reduce_end(0, v_one, radix_one)
     reduce_start(1, v_two, radix_two, radix_one, share)
-    lax.fori_loop(part_groups, groups, local, 0)
+    lax.fori_loop(part_groups, groups, local, 0, unroll=2)
 
     def back_copy(n):
         return pltpu.make_async_remote_copy(
@@ -510,7 +511,8 @@
         store(g, 3).start()
         return c
 
-    lax.fori_loop(0, groups, one, 0)
+    for g in range(groups):
+        one(g, 0)
 
     spread = jnp.broadcast_to(total_ref[...], (groups, LANES))
     own = lax.div(iota((groups, LANES), 1), MODES) == iota((groups, LANES), 0)

time: 31.7 us -> 31.4 us (level)
  no operation moved by 1% of the time
where the time goes in v5:
time: 31.4 us; the launch traced here: 31.3 us
  Pallas kernels  30.7 us (98%)
  between operations  0.64 us (2%)
    pallas_call x1, Pallas kernels, exchange(): pl.pallas_call(body, out_shape=(jax.ShapeDtypeStruct((rows, LANES), f32),...  26.9 us
    pallas_call x1, Pallas kernels, finish(): pl.pallas_call(body, out_shape=(big, big, big, big, jax.ShapeDtypeStruct(...  3.76 us

profile of v5, /device:TPU:1, one launch (start us, length us, event | category | flops | bytes accessed | tf_op | source)
XLA Modules:
  0.0 31.3 jit_solution(13501344963036270813)
XLA Ops:
  0.6 26.9 %shard_map.101 = (f32[1024,128]{1,0:T(8,128)S(1)}, f32[1,128]{1,0:T(1,128)S(1)}, bf16[4,8,128,512]{3,2,1,0:T(8,128)(2,1)S(1)}, f32[8,128,512]{2,1,0:T(8,128)S(1)...) custom-call(bf16[128,4096]{1,0:T(8,128)(2,1)} %refs_0_.1, ...), custom_call_target="tpu_custom_call" | custom-call | tf_op jit(solution)/shard_map/pallas_call | solution.py:428
  27.6 3.8 %shard_map.102 = (f32[128,4096]{1,0:T(8,128)}, f32[128,4096]{1,0:T(8,128)}, f32[128,4096]{1,0:T(8,128)}, f32[128,4096]{1,0:T(8,128)}, f32[8,16]{1,0:T(8,128)}) custom-call(f32[1024,128]{1,0:T(8,128)S(1)} %get-tuple-element.12.refs_0_, f32[1,128]{1,0:T(1,128)S(1)} %get-tuple-element.13.refs_1_, bf16[4,8,128,512]{3,2,1,0:T(8,128)(2,1)S(1)} %get-tuple-element.14.refs_2_, ...), custom_call_target="tpu_custom_call" | custom-call | tf_op jit(solution)/shard_map/pallas_call | solution.py:543

commit v6 on v5

--- a/solution.py
+++ b/solution.py
@@ -339,8 +339,10 @@
     pooled = jnp.sum(jnp.exp(-rate) * acc, axis=0, keepdims=True)
     for t in range(chips):
         back[t, TILE : TILE + 1, :] = pooled
-    for _, t in peers:
-        message(back.at[t], half.at[chip], t, sems.at[2], plane_sem.at[z]).start()
+    for d in FAR_PLANES:
+        for shift, t in peers:
+            if shift[0] == d:
+                message(back.at[t], half.at[chip], t, sems.at[2], plane_sem.at[z]).start()
     half[chip] = back[chip]
 
     share = reduce_end(0, v_one, radix_one)

time: 31.4 us -> 31.2 us (level)
  no operation moved by 1% of the time
where the time goes in v6:
time: 31.2 us; the launch traced here: 31.1 us
  Pallas kernels  30.5 us (98%)
  between operations  0.64 us (2%)
    pallas_call x1, Pallas kernels, exchange(): pl.pallas_call(body, out_shape=(jax.ShapeDtypeStruct((rows, LANES), f32),...  26.7 us
    pallas_call x1, Pallas kernels, finish(): pl.pallas_call(body, out_shape=(big, big, big, big, jax.ShapeDtypeStruct(...  3.76 us

profile of v6, /device:TPU:1, one launch (start us, length us, event | category | flops | bytes accessed | tf_op | source)
XLA Modules:
  0.0 31.1 jit_solution(12054961958191158988)
XLA Ops:
  0.6 26.7 %shard_map.101 = (f32[1024,128]{1,0:T(8,128)S(1)}, f32[1,128]{1,0:T(1,128)S(1)}, bf16[4,8,128,512]{3,2,1,0:T(8,128)(2,1)S(1)}, f32[8,128,512]{2,1,0:T(8,128)S(1)...) custom-call(bf16[128,4096]{1,0:T(8,128)(2,1)} %refs_0_.1, ...), custom_call_target="tpu_custom_call" | custom-call | tf_op jit(solution)/shard_map/pallas_call | solution.py:430
  27.4 3.8 %shard_map.102 = (f32[128,4096]{1,0:T(8,128)}, f32[128,4096]{1,0:T(8,128)}, f32[128,4096]{1,0:T(8,128)}, f32[128,4096]{1,0:T(8,128)}, f32[8,16]{1,0:T(8,128)}) custom-call(f32[1024,128]{1,0:T(8,128)S(1)} %get-tuple-element.12.refs_0_, f32[1,128]{1,0:T(1,128)S(1)} %get-tuple-element.13.refs_1_, bf16[4,8,128,512]{3,2,1,0:T(8,128)(2,1)S(1)} %get-tuple-element.14.refs_2_, ...), custom_call_target="tpu_custom_call" | custom-call | tf_op jit(solution)/shard_map/pallas_call | solution.py:545
